TPU v7x, 512 devices: a whole 4x8x8 slice. The times are simulated.
512 devices in a mesh: expert: 8 (over z), dp: 16 (over y, core), section: 4 (over x).
Axes of the slice: x: 4, y: 8, z: 8, core: 2. Of those that a mesh axis runs over, the one named last changes fastest.
Arguments:
- active: bfloat16 [4, 4096, 2, 8192], P('section', ('expert', 'dp')), may hold values from -6 to 6
- out_grad: bfloat16 [4, 4096, 3072], P('section', ('expert', 'dp')), may hold values from -6 to 6
- proj_model: bfloat16 [64, 3072], P(None, 'dp'), may hold values from -0.109375 to 0.109375
- routes: int32 [4, 4096, 2], P('section', ('expert', 'dp')), may hold values from 0 to 7, all different within a row; in each aligned block of 32 rows (0 to 31, 32 to 63, ..., all dimensions but the last counted through in order) at most 16 rows name the same one
- route_weight: float32 [4, 4096, 2], P('section', ('expert', 'dp')), may hold values from 0.2 to 1
- seq_ids: int32 [4096], P(('expert', 'dp')), may hold values from 0 to 63, never falling along the last dimension, each value on 1 to 128 neighbouring positions
- proj_hidden: bfloat16 [8, 64, 8192], P('expert', None, 'dp'), may hold values from -0.0625 to 0.0625
- query_feat: bfloat16 [4, 8, 256, 4096], P('section', 'expert', 'dp'), may hold values from -0.00390625 to 0.00390625
Outputs:
- scores: float32 [64, 256], P(('expert', 'section'), 'dp')
Inputs may be any that keep to these rules, and one draw needn't show every extreme that they name: `routes`: each row names 2 different experts; among the 32 rows of one device at one checkpoint no expert is named by more than 16 rows, and in some device's rows one expert is named by exactly 16 rows. `seq_ids`: sequence numbers never fall along the tokens; each sequence has 1 to 128 tokens, one exactly 128.
All inputs are finite; a program needn't handle non-finite values.
Results may differ from a plain program's by a relative error of at most 0.0029.
Values may be sent and summed in bfloat16 or wider, within the bound.
No kernel may reach another device: no remote copies, remote signals or barrier semaphores. Data moves between devices by JAX's collectives and lax.ppermute only.
A program may use at most 64 MiB of HBM per device.

v0:
```python
import math

import jax
import jax.numpy as jnp
from jax import lax
from jax.sharding import PartitionSpec as P

SEQS = 64


def slot_table(route_block, experts, capacity):
    flat = route_block.reshape(-1)
    pairs = flat.shape[0]
    labels = jnp.arange(experts, dtype=jnp.int32)
    member = (flat[:, None] == labels[None, :]).astype(jnp.int32)
    before = jnp.cumsum(member, axis=0) - member
    position = jnp.sum(before * member, axis=1)
    slots = jnp.arange(capacity, dtype=jnp.int32)
    match = (flat[None, None, :] == labels[:, None, None]) & (
        position[None, None, :] == slots[None, :, None]
    )
    filled = jnp.any(match, axis=2)
    slot_index = jnp.sum(
        match.astype(jnp.int32) * jnp.arange(pairs, dtype=jnp.int32)[None, None, :], axis=2
    )
    return (slot_index, filled)


def seq_features(projected, vectors, sequence_rows, sequences):
    total_rows, rank = projected.shape
    block = math.gcd(total_rows, 256)
    labels = jnp.arange(sequences, dtype=jnp.int32)

    def step(running, begin):
        vector_part = vectors.astype(jnp.float32)
        member = (sequence_rows[:, None] == labels[None, :]).astype(jnp.float32)
        outer = (projected[:, :, None] * vector_part[:, None, :]).reshape(block, rank * rank)
        added = lax.dot_general(
            member, outer, (((0,), (0,)), ((), ())), precision=lax.Precision.HIGHEST
        )
        return (running + added, None)

    begins = jnp.arange(total_rows // block, dtype=jnp.int32) * block
    running, unused = lax.scan(step, jnp.zeros((sequences, rank * rank), jnp.float32), begins)
    return running


def on_device(active, out_grad, proj_model, routes, route_weight, seq_ids, proj_hidden, query_feat):
    experts = lax.axis_size("expert")
    holders = lax.axis_size("dp")
    tok_count = active.shape[1]
    top_count = active.shape[2]
    hidden_width = active.shape[3]
    rank = proj_model.shape[0]
    spread = experts * holders
    capacity = min(tok_count, holders * ((2 * top_count * tok_count + spread - 1) // spread))
    per_holder = capacity // holders
    model_full, hidden_full = (
        lax.all_gather(proj_model, "dp", axis=1, tiled=True),
        lax.all_gather(proj_hidden[0], "dp", axis=1, tiled=True),
    )
    dy_proj = lax.dot_general(
        out_grad[0], model_full, (((1,), (1,)), ((), ())), preferred_element_type=jnp.float32
    )
    scaled = (route_weight[0][:, :, None] * dy_proj[:, None, :]).astype(jnp.bfloat16)
    slot_index, filled = slot_table(routes[0], experts, capacity)
    pair_rows = active[0].reshape(-1, hidden_width)[slot_index]
    pair_vec = jnp.where(
        filled[:, :, None], scaled.reshape(-1, rank)[slot_index], jnp.zeros((), jnp.bfloat16)
    )
    pair_seq = seq_ids[slot_index // top_count]
    lead = (experts * holders, per_holder)
    moved_a, moved_v, moved_s = (
        lax.all_to_all(
            pair_rows.reshape(lead + (hidden_width,)),
            ("expert", "dp"),
            split_axis=0,
            concat_axis=0,
            tiled=True,
        ),
        lax.all_to_all(
            pair_vec.reshape(lead + (rank,)),
            ("expert", "dp"),
            split_axis=0,
            concat_axis=0,
            tiled=True,
        ),
        lax.all_to_all(
            pair_seq.reshape(lead), ("expert", "dp"), split_axis=0, concat_axis=0, tiled=True
        ),
    )
    act_rows = lax.dot_general(
        moved_a.reshape(-1, hidden_width),
        hidden_full,
        (((1,), (1,)), ((), ())),
        preferred_element_type=jnp.float32,
    )
    vector_rows = moved_v.reshape(-1, rank)
    sequence_rows = moved_s.reshape(-1)
    partial_feat = seq_features(act_rows, vector_rows, sequence_rows, SEQS)
    queries_here = query_feat[0, 0]
    partial_scores = lax.dot_general(
        partial_feat,
        lax.all_gather(queries_here, "dp", axis=0, tiled=True).astype(jnp.float32),
        (((1,), (1,)), ((), ())),
        precision=lax.Precision.HIGHEST,
    )
    shared = lax.psum_scatter(partial_scores, "dp", scatter_dimension=1, tiled=True)
    return lax.psum_scatter(shared, ("expert", "section"), scatter_dimension=0, tiled=True)


def solution(mesh):
    placed = (
        P("section", ("expert", "dp"), None, None),
        P("section", ("expert", "dp"), None),
        P(None, "dp"),
        P("section", ("expert", "dp"), None),
        P("section", ("expert", "dp"), None),
        P(("expert", "dp")),
        P("expert", None, "dp"),
        P("section", "expert", "dp", None),
    )
    return jax.shard_map(
        on_device,
        mesh=mesh,
        in_specs=placed,
        out_specs=P(("expert", "section"), "dp"),
        check_vma=False,
    )
```

profile of v0, /device:TPU:32, one launch (start us, length us, event | category | flops | bytes accessed | tf_op | source)
XLA Modules:
  0.0 300.5 jit_solution(10034062944627521986)
XLA Ops:
  6.5 0.0 copy-start
  6.5 0.0 copy-start.1
  6.5 0.0 all-gather.6.cloned.1.call-start
  6.5 0.7 all-gather.6.cloned.1.call-update
  7.3 0.8 copy.34
  8.0 0.1 eq.73
  8.1 0.1 fusion.13
  8.2 0.1 reduce_window_sum.11
  8.3 0.2 select_reduce_fusion
  8.5 0.2 fusion.8
  8.8 0.1 reshape.182
  8.8 0.0 copy-done.1
  8.9 0.0 copy-start.3
  8.9 1.2 gather_fusion
  10.1 0.0 copy-start.4
  10.1 0.0 copy-start.2
  10.1 0.7 copy.35
  10.8 17.0 %all-to-all-start = ((s32[128,1,1]{2,1,0:T(1,128)}), s32[128,1,1]{2,1,0:T(1,128)S(1)}, u32[]{:S(2)}, u32[]{:S(2)}) async-start(s32[128,1,1]{2,1,0:T(1,128)} %copy.35), calls=%async_computation | async-start | bytes 131072 | tf_op jit(solution)/shard_map/all_to_all | solution.py:88
  27.9 0.0 copy-done.3
  27.9 16.2 %all-gather.2 = bf16[16,192,64]{1,2,0:T(8,128)(2,1)S(1)} all-gather(bf16[1,192,64]{1,2,0:T(8,128)(2,1)S(1)} %bitcast.58), channel_id=1, replica_groups=mesh['expert'=8,'dp'=16,'section'=4] {'dp'}, dimensions={0}, use_global_device_ids=true | all-gather | bytes 417792 | tf_op jit(solution)/shard_map/all_gather | solution.py:59
  44.1 0.2 and_reduce_fusion
  44.3 0.1 reshape.190
  44.4 0.3 copy.38
  44.7 0.5 reshape.213
  45.3 0.0 copy-done.4
  45.3 0.1 copy.37
  45.4 0.1 mul.62
  45.5 0.1 broadcast_in_dim.13
  45.6 0.0 copy-done
  45.6 0.2 fusion.6
  45.8 0.1 multiply_convert_fusion
  45.9 0.7 gather_fusion.2
  46.6 0.1 bitcast_select_fusion
  46.7 0.7 copy.39
  47.4 0.0 all-to-all-done
  47.4 13.9 %all-to-all-start.2 = ((bf16[128,1,64]{2,1,0:T(2,128)(2,1)}), bf16[128,1,64]{2,1,0:T(2,128)(2,1)S(1)}, u32[]{:S(2)}, u32[]{:S(2)}) async-start(bf16[128,1,64]{2,1,0:T(2,128)(2,1)} %copy.39), calls=%async_computation.2 | async-start | bytes 131072 | tf_op jit(solution)/shard_map/all_to_all | solution.py:81
  61.3 0.0 copy-done.2
  61.3 0.4 reshape_squeeze.3
  61.8 1.9 gather_fusion.1
  63.6 0.5 broadcast.161
  64.1 2.9 reduce.1
  67.0 4.5 %reshape.218 = bf16[128,2,4096]{2,1,0:T(2,128)(2,1)} reshape(bf16[128,8192]{1,0:T(8,128)(2,1)} %reduce.1) | data formatting | bytes 4194304
  71.5 0.0 all-to-all-done.2
  71.5 13.7 %all-to-all-start.1 = ((bf16[128,2,4096]{2,1,0:T(2,128)(2,1)}), bf16[128,2,4096]{2,1,0:T(2,128)(2,1)S(1)}, u32[]{:S(2)}, u32[]{:S(2)}) async-start(bf16[128,2,4096]{2,1,0:T(2,128)(2,1)} %reshape.218), calls=%async_computation.1 | async-start | bytes 4194304 | tf_op jit(solution)/shard_map/all_to_all | solution.py:74
  85.2 0.0 all-gather.8.cloned.1.call-start
  85.3 0.7 all-gather.8.cloned.1.call-update
  86.0 0.2 reduce-scatter.3.cloned.1.call-start
  86.2 2.4 reduce
  88.6 0.1 mul.72
  88.7 0.1 copy.40
  88.7 56.5 %all-to-all-done.1 = bf16[128,2,4096]{2,1,0:T(2,128)(2,1)S(1)} async-done(((bf16[128,2,4096]{2,1,0:T(2,128)(2,1)}), bf16[128,2,4096]{2,1,0:T(2,128)(2,1)S(1)}, u32[]{:S(2)}, u32[]{:S(2)}) %all-to-all-start.1) | async-done | bytes 2097184 | tf_op jit(solution)/shard_map/all_to_all | solution.py:74
  145.2 6.8 %reshape.219 = bf16[128,1,8192]{2,1,0:T(2,128)(2,1)} reshape(bf16[128,2,4096]{2,1,0:T(2,128)(2,1)S(1)} %all-to-all-done.1) | data formatting | bytes 4194304
  152.0 0.0 all-gather.6.cloned.1.call-done
  152.0 4.9 %fusion = f32[128,64]{0,1:T(8,128)S(1)} fusion(bf16[128,1,8192]{2,1,0:T(2,128)(2,1)} %reshape.219, bf16[1,64,8192]{2,1,0:T(8,128)(2,1)} %all-gather.6.cloned.1.call-done), kind=kOutput, calls=%fused_computation.3 | convolution fusion | flops 134217728 | bytes 3178496 | tf_op jit(solution)/shard_map/dot_general | solution.py:92
  156.9 0.3 broadcast_multiply_fusion
  157.2 1.4 fusion.10
  158.6 0.0 all-gather.8.cloned.1.call-done
  158.6 4.0 %fusion.3 = f32[64,256]{0,1:T(8,128)} fusion(f32[64,4096]{1,0:T(8,128)S(1)} %fusion.10, bf16[1,1,256,4096]{3,2,1,0:T(8,128)(2,1)} %all-gather.8.cloned.1.call-done), kind=kOutput, calls=%fused_computation.6 | convolution fusion | flops 805306368 | bytes 3211264 | tf_op jit(solution)/shard_map/dot_general | solution.py:102
  162.6 0.0 reduce-scatter.3.cloned.1.call-update
  162.7 1.3 dynamic-slice
  164.6 52.0 %reduce-scatter.3.cloned.1.call-done = f32[64,16]{0,1:T(8,128)} async-done(((f32[64,256]{0,1:T(8,128)}), f32[64,16]{0,1:T(8,128)}) %reduce-scatter.3.cloned.1.call-update) | async-done | bytes 4112 | tf_op jit(solution)/shard_map/reduce_scatter | solution.py:108
  216.6 76.6 %all-reduce = f32[64,16]{0,1:T(8,128)S(1)} all-reduce(f32[64,16]{0,1:T(8,128)} %reduce-scatter.3.cloned.1.call-done), channel_id=5, replica_groups=mesh['expert'=8,'dp'=16,'section'=4] {'expert','section'}, use_global_device_ids=true, to_apply=%region_5.6.clone | all-reduce | flops 1024 | bytes 8192
  293.3 0.1 constant_dynamic-slice_fusion
  293.3 0.6 copy.41
  (6 shorter events, 0.1 us)
Async XLA Ops:
  6.5 39.0 %copy-start = (bf16[1,32,3072]{2,1,0:T(8,128)(2,1)S(1)}, bf16[1,32,3072]{2,1,0:T(8,128)(2,1)}, u32[]{:S(2)}) copy-start(bf16[1,32,3072]{2,1,0:T(8,128)(2,1)} %param.9) | copy-start | bytes 589828
  6.5 2.3 copy-start.1
  6.5 145.5 %all-gather.6.cloned.1.call-start = ((), (), s32[]{:S(2)}) async-start(), calls=%async_computation.5 | async-start | bytes 1114112 | tf_op jit(solution)/shard_map/all_gather | solution.py:60
  8.9 19.0 %copy-start.3 = (bf16[64,192]{1,0:T(8,128)(2,1)S(1)}, bf16[64,192]{1,0:T(8,128)(2,1)}, u32[]{:S(2)}) copy-start(bf16[64,192]{1,0:T(8,128)(2,1)} %param.10) | copy-start | bytes 73732
  10.1 35.2 %copy-start.4 = (f32[1,32,2]{1,2,0:T(2,128)S(1)}, f32[1,32,2]{1,2,0:T(2,128)}, u32[]{:S(2)}) copy-start(f32[1,32,2]{1,2,0:T(2,128)} %param.12) | copy-start | bytes 772
  10.1 51.2 %copy-start.2 = (bf16[1,32,2,8192]{3,2,1,0:T(2,128)(2,1)S(1)}, bf16[1,32,2,8192]{3,2,1,0:T(2,128)(2,1)}, u32[]{:S(2)}) copy-start(bf16[1,32,2,8192]{3,2,1,0:T(2,128)(2,1)} %param.8) | copy-start | bytes 3145732
  10.8 36.6 %all-to-all-start = ((s32[128,1,1]{2,1,0:T(1,128)}), s32[128,1,1]{2,1,0:T(1,128)S(1)}, u32[]{:S(2)}, u32[]{:S(2)}) async-start(s32[128,1,1]{2,1,0:T(1,128)} %copy.35), calls=%async_computation | async-start | bytes 131072 | tf_op jit(solution)/shard_map/all_to_all | solution.py:88
  47.4 24.1 %all-to-all-start.2 = ((bf16[128,1,64]{2,1,0:T(2,128)(2,1)}), bf16[128,1,64]{2,1,0:T(2,128)(2,1)S(1)}, u32[]{:S(2)}, u32[]{:S(2)}) async-start(bf16[128,1,64]{2,1,0:T(2,128)(2,1)} %copy.39), calls=%async_computation.2 | async-start | bytes 131072 | tf_op jit(solution)/shard_map/all_to_all | solution.py:81
  71.5 73.7 %all-to-all-start.1 = ((bf16[128,2,4096]{2,1,0:T(2,128)(2,1)}), bf16[128,2,4096]{2,1,0:T(2,128)(2,1)S(1)}, u32[]{:S(2)}, u32[]{:S(2)}) async-start(bf16[128,2,4096]{2,1,0:T(2,128)(2,1)} %reshape.218), calls=%async_computation.1 | async-start | bytes 4194304 | tf_op jit(solution)/shard_map/all_to_all | solution.py:74
  85.2 73.4 %all-gather.8.cloned.1.call-start = ((), (), s32[]{:S(2)}) async-start(), calls=%async_computation.6 | async-start | bytes 2228224 | tf_op jit(solution)/shard_map/all_gather | solution.py:104
  86.0 130.6 %reduce-scatter.3.cloned.1.call-start = ((), (), s32[]{:S(2)}) async-start(), calls=%async_computation.4 | async-start | bytes 139264 | tf_op jit(solution)/shard_map/reduce_scatter | solution.py:108
Sparse Core Ops, SparseCore 0:
  9.5 43.3 all-gather.5
  88.2 52.9 all-gather.7
  162.8 53.7 reduce-scatter.2
where the time goes:
time: 301 us
  waiting for transfers between devices  110 us (37%)
  blocking collectives  92.9 us (31%)
  starting transfers between devices  44.9 us (15%)
  local copies, waits for them, and re-layouts  21.7 us (7%)
  between operations  14 us (5%)
  matrix products  10.5 us (3%)
  other arithmetic  6.56 us (2%)
    unnamed x1, blocking collectives  76.6 us
    all_to_all x1, waiting for transfers between devices, on_device(): lax.all_to_all(pair_rows.reshape(lead + (hidden_width,)), ('expert', 'dp'...  56.5 us
    reduce_scatter x1, waiting for transfers between devices, on_device(): lax.psum_scatter(partial_scores, 'dp', scatter_dimension=1, tiled=True)  52 us
    all_to_all x1, starting transfers between devices, on_device(): lax.all_to_all(pair_seq.reshape(lead), ('expert', 'dp'), split_axis=0, co...  17 us
    all_gather x1, blocking collectives, on_device(): lax.all_gather(proj_model, 'dp', axis=1, tiled=True)  16.2 us
    unnamed x17, local copies, waits for them, and re-layouts  14 us
    all_to_all x1, starting transfers between devices, on_device(): lax.all_to_all(pair_vec.reshape(lead + (rank,)), ('expert', 'dp'), split_...  13.9 us
    all_to_all x1, starting transfers between devices, on_device(): lax.all_to_all(pair_rows.reshape(lead + (hidden_width,)), ('expert', 'dp'...  13.7 us
  transfers between devices with their start and end apart: 6, of which 2 were waited for; matrix products, arithmetic and copies ran while one was open for 11% of the time, Pallas kernels for 0%

commit v1 on v0

v1 whole, which is shorter than its diff:
```python
import jax
import jax.numpy as jnp
from jax import lax
from jax.experimental import pallas as pl
from jax.experimental.pallas import tpu as pltpu
from jax.sharding import PartitionSpec as P

SEQS = 64
CAP = 16
F32 = jnp.float32
BF16 = jnp.bfloat16


def exchange(x, axes):
    return lax.all_to_all(x, axes, split_axis=0, concat_axis=0, tiled=True)


def dot(a, b, contract=((1,), (0,)), **kw):
    return lax.dot_general(a, b, (contract, ((), ())), preferred_element_type=F32, **kw)


def score_kernel(known_ref, q_ref, out_ref):
    holders, experts, _, lanes = known_ref.shape
    rank = lanes // 2
    queries = q_ref.shape[1] // rank
    wide = q_ref.shape[1]
    row = lax.broadcasted_iota(jnp.int32, (lanes, lanes), 0)
    col = lax.broadcasted_iota(jnp.int32, (lanes, lanes), 1)
    twice = ((row >= rank) & ((row == col) | (row == col + rank))).astype(BF16)
    owner = lax.broadcasted_iota(jnp.int32, (experts, experts * CAP), 1) // CAP
    own = owner == lax.broadcasted_iota(jnp.int32, (experts, experts * CAP), 0)
    label = lax.broadcasted_iota(jnp.int32, (SEQS, experts * CAP), 0).astype(F32)

    def step(d, total):
        block = known_ref[d]
        rows = block[:, :CAP, :].reshape(experts * CAP, lanes)
        line = block[:, CAP, :].astype(F32)
        seqs = jnp.sum(jnp.where(own, line, 0.0), axis=0, keepdims=True)
        temp = dot(rows, q_ref[...])
        vecs = dot(rows, twice)
        prod = jnp.concatenate([temp[:, i : i + lanes] * vecs for i in range(0, wide, lanes)], axis=1)
        high = prod.astype(BF16)
        low = (prod - high.astype(F32)).astype(BF16)
        sel = (label == seqs).astype(F32).astype(BF16)
        return total + (dot(sel, high) + dot(sel, low))

    total = lax.fori_loop(0, holders, step, jnp.zeros((SEQS, wide), F32))
    group = lax.broadcasted_iota(jnp.int32, (wide, lanes), 0) // rank
    ones = (group == lax.broadcasted_iota(jnp.int32, (wide, lanes), 1)).astype(F32)
    out_ref[...] = dot(total, ones, precision=lax.Precision.HIGHEST)[:, :queries]


def on_device(active, out_grad, proj_model, routes, route_weight, seq_ids, proj_hidden, query_feat):
    experts = lax.axis_size("expert")
    holders = lax.axis_size("dp")
    toks, top, hidden = active.shape[1:]
    rank = proj_model.shape[0]
    chunk = hidden // holders
    width = out_grad.shape[2] // holders
    pairs = top * toks
    half = toks // 2

    ids = routes[0].T.reshape(pairs)

    weights = proj_hidden
    order = [0]
    bit = experts // 2
    while bit:
        other = lax.ppermute(weights, "expert", [(i, i ^ bit) for i in range(experts)])
        weights = jnp.concatenate([weights, other], axis=0)
        order = order + [o ^ bit for o in order]
        bit //= 2
    me = lax.axis_index("expert")

    acts = active[0].reshape(toks, top, holders, chunk).transpose(2, 1, 0, 3).reshape(holders, pairs, chunk)
    grads = out_grad[0].reshape(toks, holders, width).transpose(1, 0, 2)
    named = jnp.broadcast_to(routes[0].astype(BF16)[None], (holders, toks, top))
    gap = jnp.zeros((holders, toks, chunk // 2 - width - top), BF16)
    side = jnp.concatenate([grads, named, gap], axis=2)
    side = jnp.concatenate([side[:, :half], side[:, half:]], axis=2)
    got = exchange(jnp.concatenate([acts, side], axis=1), "dp")

    rows = got[:, :pairs].reshape(holders * pairs, chunk)
    every = lax.dot_general(
        rows, weights.reshape(experts * rank, chunk), (((1,), (1,)), ((), ())), preferred_element_type=F32
    )
    rest = jnp.concatenate([got[:, pairs:, : chunk // 2], got[:, pairs:, chunk // 2 :]], axis=1)
    code = rest[:, :, width : width + top].transpose(0, 2, 1).reshape(holders * pairs, 1)
    part = jnp.zeros((holders * pairs, rank), F32)
    for e in range(experts):
        part = part + jnp.where(code == (me ^ order[e]).astype(BF16), every[:, e * rank : (e + 1) * rank], 0.0)
    part_dy = lax.dot_general(
        rest[:, :, :width], proj_model, (((2,), (1,)), ((), ())), preferred_element_type=F32
    )
    part = part.reshape(holders, top, toks, rank)
    send = jnp.concatenate(
        [
            jnp.concatenate([part[:, 0], part[:, 1]], axis=2),
            jnp.concatenate([part_dy[:, :half], part_dy[:, half:]], axis=2),
        ],
        axis=1,
    )
    whole = jnp.sum(exchange(send, "dp"), axis=0)
    act_proj = jnp.concatenate([whole[:toks, :rank], whole[:toks, rank:]], axis=0)
    dy_proj = jnp.concatenate([whole[toks:, :rank], whole[toks:, rank:]], axis=0)
    scaled = (route_weight[0].T[:, :, None] * dy_proj[None]).astype(BF16).reshape(pairs, rank)

    member = (ids[:, None] == jnp.arange(experts)[None, :]).astype(F32)
    before = lax.dot_general(
        jnp.tril(jnp.ones((pairs, pairs), F32), -1), member, (((1,), (0,)), ((), ())), preferred_element_type=F32
    )
    place = jnp.sum(before * member, axis=1)
    slot = ids * CAP + place.astype(jnp.int32)
    pick = (jnp.arange(experts * CAP)[:, None] == slot[None, :]).astype(BF16)
    both = jnp.concatenate([act_proj.astype(BF16), scaled], axis=1)
    slots = lax.dot_general(pick, both, (((1,), (0,)), ((), ())), preferred_element_type=F32).astype(BF16)
    pair_seq = jnp.concatenate([seq_ids] * top).astype(BF16)
    belongs = (place[:, None].astype(jnp.int32) == (jnp.arange(2 * rank) % CAP)[None, :]).astype(BF16)
    line = dot((member * jnp.concatenate([seq_ids] * top)[:, None].astype(F32)).astype(BF16), belongs, ((0,), (0,)))
    line = jnp.pad(line.astype(BF16)[:, None], ((0, 0), (0, 7), (0, 0)))
    moved = exchange(jnp.concatenate([slots.reshape(experts, CAP, 2 * rank), line], axis=1), "expert")
    known = lax.all_gather(moved, "dp", axis=0, tiled=False)

    queries = query_feat.shape[2]
    q = query_feat[0, 0].reshape(queries, rank, rank).transpose(1, 0, 2).reshape(rank, queries * rank)
    q = jnp.pad(q, ((0, rank), (0, 0)))
    scores = pl.pallas_call(
        score_kernel,
        out_shape=jax.ShapeDtypeStruct((SEQS, queries), F32),
        in_specs=[pl.BlockSpec(memory_space=pltpu.VMEM)] * 2,
        out_specs=pl.BlockSpec(memory_space=pltpu.VMEM),
        name="score",
    )(known, q)
    sections = lax.axis_size("section")
    out = exchange(scores.reshape(experts * sections, SEQS // (experts * sections), queries), ("expert", "section"))
    return jnp.sum(out, axis=0)


def solution(mesh):
    placed = (
        P("section", ("expert", "dp"), None, None),
        P("section", ("expert", "dp"), None),
        P(None, "dp"),
        P("section", ("expert", "dp"), None),
        P("section", ("expert", "dp"), None),
        P(("expert", "dp")),
        P("expert", None, "dp"),
        P("section", "expert", "dp", None),
    )
    return jax.shard_map(
        on_device,
        mesh=mesh,
        in_specs=placed,
        out_specs=P(("expert", "section"), "dp"),
        check_vma=False,
    )
```

time: 301 us -> 134 us (0.45)
  the two profiles are of different devices: /device:TPU:32 before, /device:TPU:1 now
where the time goes in v1:
time: 134 us; the launch traced here: 133 us
  starting transfers between devices  40.4 us (30%)
  waiting for transfers between devices  36.9 us (28%)
  blocking collectives  31.4 us (23%)
  Pallas kernels  10.2 us (8%)
  local copies, waits for them, and re-layouts  7.26 us (5%)
  other arithmetic  5.07 us (4%)
  matrix products  1.55 us (1%)
    all_to_all x3, starting transfers between devices, exchange(): return lax.all_to_all(x, axes, split_axis=0, concat_axis=0, tiled=True)  23.9 us
    all_to_all x3, waiting for transfers between devices, exchange(): return lax.all_to_all(x, axes, split_axis=0, concat_axis=0, tiled=True)  21.1 us
    all_gather x1, blocking collectives, on_device(): known = lax.all_gather(moved, 'dp', axis=0, tiled=False)  18.2 us
    ppermute x3, starting transfers between devices, on_device(): lax.ppermute(weights, 'expert', [(i, i ^ bit) for i in range(experts)])  16.5 us
    ppermute x3, waiting for transfers between devices, on_device(): lax.ppermute(weights, 'expert', [(i, i ^ bit) for i in range(experts)])  15.8 us
    all_to_all x1, blocking collectives, exchange(): return lax.all_to_all(x, axes, split_axis=0, concat_axis=0, tiled=True)  13.2 us
    pallas_call x1, Pallas kernels, on_device(): pl.pallas_call(score_kernel, out_shape=jax.ShapeDtypeStruct((SEQS, querie...  10.2 us
  transfers between devices with their start and end apart: 6, of which 6 were waited for; matrix products, arithmetic and copies ran while one was open for 2% of the time, Pallas kernels for 0%

profile of v1, /device:TPU:1, one launch (start us, length us, event | category | flops | bytes accessed | tf_op | source)
XLA Modules:
  0.0 133.2 jit_solution(5383053855875654353)
XLA Ops:
  0.0 1.3 %reshape_squeeze.10 = bf16[32,16,192]{2,1,0:T(8,128)(2,1)S(1)} reshape(bf16[1,32,3072]{2,1,0:T(8,128)(2,1)} %param.9) | data formatting | bytes 393216 | tf_op jit(solution)/shard_map/reshape;squeeze | solution.py:76
  1.4 0.1 copy.50
  1.4 0.7 convert_bitcast_fusion
  2.1 0.1 copy.32
  2.2 0.1 pad.39.clone
  2.3 0.1 maximum_maximum_fusion.2
  2.5 0.8 reshape_squeeze.9
  3.3 0.6 copy.30
  3.9 1.2 maximum_maximum_fusion
  5.1 10.5 %all-to-all-start = ((bf16[16,80,512]{2,1,0:T(8,128)(2,1)}), bf16[16,80,512]{2,1,0:T(8,128)(2,1)S(1)}, u32[]{:S(2)}, u32[]{:S(2)}) async-start(bf16[16,80,512]{2,1,0:T(8,128)(2,1)} %maximum_maximum_fusion), calls=%async_computation | async-start | bytes 2621440 | tf_op jit(solution)/shard_map/all_to_all | solution.py:15
  15.5 8.9 %collective-permute-start = (bf16[1,64,512]{2,1,0:T(8,128)(2,1)S(1)}, bf16[1,64,512]{2,1,0:T(8,128)(2,1)S(1)}, u32[]{:S(2)}, u32[]{:S(2)}) collective-permute-start(bf16[1,64,512]{2,1,0:T(8,128)(2,1)S(1)} %copy-done.2), channel_id=1, source_target_pairs={{0,256},{64,320},{128,384},{192,448},{256,0},{320,64},{384,128},{4... | collective-permute-start | bytes 196616 | tf_op jit(solution)/shard_map/ppermute | solution.py:69
  24.5 2.4 %collective-permute-done = bf16[1,64,512]{2,1,0:T(8,128)(2,1)S(1)} collective-permute-done((bf16[1,64,512]{2,1,0:T(8,128)(2,1)S(1)}, bf16[1,64,512]{2,1,0:T(8,128)(2,1)S(1)}, u32[]{:S(2)}, u32[]{:S(2)}) %collective-permute-start) | collective-permute-done | bytes 65568 | tf_op jit(solution)/shard_map/ppermute | solution.py:69
  26.8 5.7 %collective-permute-start.1 = (bf16[2,64,512]{2,1,0:T(8,128)(2,1)S(1)}, bf16[2,64,512]{2,1,0:T(8,128)(2,1)S(1)}, u32[]{:S(2)}, u32[]{:S(2)}) collective-permute-start(bf16[2,64,512]{2,1,0:T(8,128)(2,1)S(1)} %pad_maximum_fusion.4), channel_id=1, source_target_pairs={{0,128},{64,192},{128,0},{192,64},{256,384},{320,448},{384,256},{4... | collective-permute-start | bytes 393224 | tf_op jit(solution)/shard_map/ppermute | solution.py:69
  32.5 6.3 %collective-permute-done.1 = bf16[2,64,512]{2,1,0:T(8,128)(2,1)S(1)} collective-permute-done((bf16[2,64,512]{2,1,0:T(8,128)(2,1)S(1)}, bf16[2,64,512]{2,1,0:T(8,128)(2,1)S(1)}, u32[]{:S(2)}, u32[]{:S(2)}) %collective-permute-start.1) | collective-permute-done | bytes 131104 | tf_op jit(solution)/shard_map/ppermute | solution.py:69
  38.8 1.9 %collective-permute-start.2 = (bf16[4,64,512]{2,1,0:T(8,128)(2,1)S(1)}, bf16[4,64,512]{2,1,0:T(8,128)(2,1)S(1)}, u32[]{:S(2)}, u32[]{:S(2)}) collective-permute-start(bf16[4,64,512]{2,1,0:T(8,128)(2,1)S(1)} %pad_maximum_fusion.3), channel_id=1, source_target_pairs={{0,64},{64,0},{128,192},{192,128},{256,320},{320,256},{384,448},{4... | collective-permute-start | bytes 786440 | tf_op jit(solution)/shard_map/ppermute | solution.py:69
  40.8 0.1 mul.42
  40.9 0.1 reshape.142
  41.0 7.1 %collective-permute-done.2 = bf16[4,64,512]{2,1,0:T(8,128)(2,1)S(1)} collective-permute-done((bf16[4,64,512]{2,1,0:T(8,128)(2,1)S(1)}, bf16[4,64,512]{2,1,0:T(8,128)(2,1)S(1)}, u32[]{:S(2)}, u32[]{:S(2)}) %collective-permute-start.2) | collective-permute-done | bytes 262176 | tf_op jit(solution)/shard_map/ppermute | solution.py:69
  48.1 0.1 pad_maximum_fusion
  48.2 0.7 all-to-all-done
  48.9 0.1 compare_bitcast_fusion.7
  49.0 0.2 compare_bitcast_fusion.6
  49.2 0.2 copy.34
  49.4 0.1 eq.190
  49.5 0.2 copy.35
  49.7 0.1 eq.194
  49.8 0.2 copy.36
  50.0 0.1 eq.198
  50.1 0.2 copy.37
  50.3 0.1 eq.202
  50.3 0.2 copy.38
  50.5 0.1 eq.206
  50.6 0.2 copy.39
  50.8 0.1 eq.210
  50.9 0.2 copy.40
  51.1 0.1 eq.214
  51.2 0.2 copy.33
  51.4 0.1 eq.186
  51.5 0.1 slice.100
  51.6 0.7 fusion.44
  52.3 0.2 fusion.4
  52.5 0.2 copy.41
  52.8 0.2 fusion.2
  53.0 0.9 maximum_maximum_fusion.1
  54.0 7.2 %all-to-all-start.1 = ((f32[16,48,128]{2,1,0:T(8,128)}), f32[16,48,128]{2,1,0:T(8,128)S(1)}, u32[]{:S(2)}, u32[]{:S(2)}) async-start(f32[16,48,128]{2,1,0:T(8,128)} %maximum_maximum_fusion.1), calls=%async_computation.1 | async-start | bytes 786432 | tf_op jit(solution)/shard_map/all_to_all | solution.py:15
  61.2 0.2 fusion
  61.4 0.1 add_convert_fusion
  61.5 0.2 fusion.1
  61.7 14.0 %all-to-all-done.1 = f32[16,48,128]{2,1,0:T(8,128)S(1)} async-done(((f32[16,48,128]{2,1,0:T(8,128)}), f32[16,48,128]{2,1,0:T(8,128)S(1)}, u32[]{:S(2)}, u32[]{:S(2)}) %all-to-all-start.1) | async-done | bytes 393248 | tf_op jit(solution)/shard_map/all_to_all | solution.py:15
  75.7 0.1 fusion.42
  75.8 0.1 fusion.43
  75.9 0.1 fusion.14
  75.9 0.2 convolution_convert_fusion
  76.1 0.6 fusion.13
  76.8 6.3 %all-to-all-start.2 = ((bf16[8,24,128]{2,1,0:T(8,128)(2,1)}), bf16[8,24,128]{2,1,0:T(8,128)(2,1)S(1)}, u32[]{:S(2)}, u32[]{:S(2)}) async-start(bf16[8,24,128]{2,1,0:T(8,128)(2,1)} %fusion.13), calls=%async_computation.2 | async-start | bytes 98304 | tf_op jit(solution)/shard_map/all_to_all | solution.py:15
  83.1 0.2 reshape_squeeze.11
  83.3 0.2 copy.49
  83.5 0.2 reshape.148
  83.7 0.7 pad.9.q_ref
  84.4 6.5 %all-to-all-done.2 = bf16[8,24,128]{2,1,0:T(8,128)(2,1)S(1)} async-done(((bf16[8,24,128]{2,1,0:T(8,128)(2,1)}), bf16[8,24,128]{2,1,0:T(8,128)(2,1)S(1)}, u32[]{:S(2)}, u32[]{:S(2)}) %all-to-all-start.2) | async-done | bytes 49184 | tf_op jit(solution)/shard_map/all_to_all | solution.py:15
  90.9 18.2 %all-gather = bf16[128,24,128]{2,1,0:T(8,128)(2,1)} all-gather(bf16[8,24,128]{2,1,0:T(8,128)(2,1)S(1)} %all-to-all-done.2), channel_id=2, replica_groups=mesh['expert'=8,'dp'=16,'section'=4] {'dp'}, dimensions={0}, use_global_device_ids=true | all-gather | bytes 835584 | tf_op jit(solution)/shard_map/all_gather | solution.py:122
  109.1 10.2 %score.1 = f32[64,16]{1,0:T(8,128)} custom-call(bf16[16,8,24,128]{3,2,1,0:T(8,128)(2,1)} %bitcast.60, bf16[128,1024]{1,0:T(8,128)(2,1)} %pad.9.q_ref), custom_call_target="tpu_custom_call" | custom-call | tf_op jit(solution)/shard_map/score/pallas_call | solution.py:127
  119.4 13.2 %all_to_all.20 = f32[32,2,16]{2,1,0:T(2,128)S(1)} all-to-all(f32[32,2,16]{2,1,0:T(2,128)} %bitcast.65), channel_id=1, replica_groups=mesh['expert'=8,'dp'=16,'section'=4] {'expert','section'}, dimensions={0} | all-to-all | bytes 8192 | tf_op jit(solution)/shard_map/all_to_all | solution.py:15
  132.6 0.6 reduce_sum.29
  (30 shorter events, 0.3 us)
Async XLA Ops:
  0.0 52.8 %copy-start = (bf16[64,192]{1,0:T(8,128)(2,1)S(1)}, bf16[64,192]{1,0:T(8,128)(2,1)}, u32[]{:S(2)}) copy-start(bf16[64,192]{1,0:T(8,128)(2,1)} %param.10) | copy-start | bytes 73732
  0.0 2.5 %copy-start.1 = (bf16[1,32,2,8192]{3,2,1,0:T(2,128)(2,1)S(1)}, bf16[1,32,2,8192]{3,2,1,0:T(2,128)(2,1)}, u32[]{:S(2)}) copy-start(bf16[1,32,2,8192]{3,2,1,0:T(2,128)(2,1)} %param.8) | copy-start | bytes 3145732
  3.9 11.7 %copy-start.2 = (bf16[1,64,512]{2,1,0:T(8,128)(2,1)S(1)}, bf16[1,64,512]{2,1,0:T(8,128)(2,1)}, u32[]{:S(2)}) copy-start(bf16[1,64,512]{2,1,0:T(8,128)(2,1)} %param.14) | copy-start | bytes 196612
  5.1 35.7 %copy-start.4 = (f32[1,32,2]{1,2,0:T(2,128)S(1)}, f32[1,32,2]{1,2,0:T(2,128)}, u32[]{:S(2)}) copy-start(f32[1,32,2]{1,2,0:T(2,128)} %param.12) | copy-start | bytes 772
  5.1 35.8 %copy-start.5 = (s32[1,32,2]{1,2,0:T(2,128)S(1)}, s32[1,32,2]{1,2,0:T(2,128)}, u32[]{:S(2)}) copy-start(s32[1,32,2]{1,2,0:T(2,128)} %param.11) | copy-start | bytes 772
  5.1 43.8 %all-to-all-start = ((bf16[16,80,512]{2,1,0:T(8,128)(2,1)}), bf16[16,80,512]{2,1,0:T(8,128)(2,1)S(1)}, u32[]{:S(2)}, u32[]{:S(2)}) async-start(bf16[16,80,512]{2,1,0:T(8,128)(2,1)} %maximum_maximum_fusion), calls=%async_computation | async-start | bytes 2621440 | tf_op jit(solution)/shard_map/all_to_all | solution.py:15
  15.5 11.3 %collective-permute-start = (bf16[1,64,512]{2,1,0:T(8,128)(2,1)S(1)}, bf16[1,64,512]{2,1,0:T(8,128)(2,1)S(1)}, u32[]{:S(2)}, u32[]{:S(2)}) collective-permute-start(bf16[1,64,512]{2,1,0:T(8,128)(2,1)S(1)} %copy-done.2), channel_id=1, source_target_pairs={{0,256},{64,320},{128,384},{192,448},{256,0},{320,64},{384,128},{4... | collective-permute-start | bytes 196616 | tf_op jit(solution)/shard_map/ppermute | solution.py:69
  26.8 12.0 %collective-permute-start.1 = (bf16[2,64,512]{2,1,0:T(8,128)(2,1)S(1)}, bf16[2,64,512]{2,1,0:T(8,128)(2,1)S(1)}, u32[]{:S(2)}, u32[]{:S(2)}) collective-permute-start(bf16[2,64,512]{2,1,0:T(8,128)(2,1)S(1)} %pad_maximum_fusion.4), channel_id=1, source_target_pairs={{0,128},{64,192},{128,0},{192,64},{256,384},{320,448},{384,256},{4... | collective-permute-start | bytes 393224 | tf_op jit(solution)/shard_map/ppermute | solution.py:69
  38.8 9.3 %collective-permute-start.2 = (bf16[4,64,512]{2,1,0:T(8,128)(2,1)S(1)}, bf16[4,64,512]{2,1,0:T(8,128)(2,1)S(1)}, u32[]{:S(2)}, u32[]{:S(2)}) collective-permute-start(bf16[4,64,512]{2,1,0:T(8,128)(2,1)S(1)} %pad_maximum_fusion.3), channel_id=1, source_target_pairs={{0,64},{64,0},{128,192},{192,128},{256,320},{320,256},{384,448},{4... | collective-permute-start | bytes 786440 | tf_op jit(solution)/shard_map/ppermute | solution.py:69
  52.7 8.7 %copy-start.6 = (s32[32]{0:T(128)S(1)}, s32[32]{0:T(128)}, u32[]{:S(2)}) copy-start(s32[32]{0:T(128)} %param.13) | copy-start | bytes 388
  52.8 30.3 %copy-start.3 = (bf16[1,1,16,4096]{3,2,1,0:T(8,128)(2,1)S(1)}, bf16[1,1,16,4096]{3,2,1,0:T(8,128)(2,1)}, u32[]{:S(2)}) copy-start(bf16[1,1,16,4096]{3,2,1,0:T(8,128)(2,1)} %param.15) | copy-start | bytes 393220
  54.0 21.7 %all-to-all-start.1 = ((f32[16,48,128]{2,1,0:T(8,128)}), f32[16,48,128]{2,1,0:T(8,128)S(1)}, u32[]{:S(2)}, u32[]{:S(2)}) async-start(f32[16,48,128]{2,1,0:T(8,128)} %maximum_maximum_fusion.1), calls=%async_computation.1 | async-start | bytes 786432 | tf_op jit(solution)/shard_map/all_to_all | solution.py:15
  76.8 14.1 %all-to-all-start.2 = ((bf16[8,24,128]{2,1,0:T(8,128)(2,1)}), bf16[8,24,128]{2,1,0:T(8,128)(2,1)S(1)}, u32[]{:S(2)}, u32[]{:S(2)}) async-start(bf16[8,24,128]{2,1,0:T(8,128)(2,1)} %fusion.13), calls=%async_computation.2 | async-start | bytes 98304 | tf_op jit(solution)/shard_map/all_to_all | solution.py:15

commit v2 on v1

v2 whole, which is shorter than its diff:
```python
import jax
import jax.numpy as jnp
from jax import lax
from jax.experimental import pallas as pl
from jax.experimental.pallas import tpu as pltpu
from jax.sharding import PartitionSpec as P

SEQS = 64
CAP = 16
LANES = 128
ROOM = 20 << 20
F32 = jnp.float32
BF16 = jnp.bfloat16
VMEM = pl.BlockSpec(memory_space=pltpu.VMEM)
SMEM = pl.BlockSpec(memory_space=pltpu.SMEM)


def exchange(x, axes):
    return lax.all_to_all(x, axes, split_axis=0, concat_axis=0, tiled=True)


def dot(a, b, contract=((1,), (0,)), **kw):
    return lax.dot_general(a, b, (contract, ((), ())), preferred_element_type=F32, **kw)


def iota(shape, axis):
    return lax.broadcasted_iota(jnp.int32, shape, axis)


def call(kernel, name, shape, dtype, *args):
    specs = [SMEM if a.ndim == 1 else VMEM for a in args]
    return pl.pallas_call(
        kernel,
        name=name,
        out_shape=jax.ShapeDtypeStruct(shape, dtype),
        in_specs=specs,
        out_specs=VMEM,
        compiler_params=pltpu.CompilerParams(vmem_limit_bytes=ROOM),
    )(*args)


def pack_kernel(acts_ref, grads_ref, routes_ref, out_ref):
    holders, _, chunk = out_ref.shape
    pairs = acts_ref.shape[0]
    toks, feats = grads_ref.shape
    width = feats // holders
    half = toks // 2
    token, lane = iota((toks, LANES), 0), iota((toks, LANES), 1) % pairs
    named = routes_ref[...].astype(F32).astype(BF16)
    first = dot(named, (lane == 2 * token).astype(F32).astype(BF16))
    second = dot(named, (lane == 2 * token + 1).astype(F32).astype(BF16))
    code = jnp.broadcast_to(first[0:1] + second[1:2], (toks, LANES))
    low = iota((toks, LANES), 1) < width % LANES
    for j in range(holders):
        out_ref[j, :pairs, :] = acts_ref[:, j * chunk : (j + 1) * chunk]
        base = width * j // LANES * LANES
        left = grads_ref[:, base : base + LANES]
        right = grads_ref[:, base + LANES : base + 2 * LANES]
        if width * j == base:
            right = jnp.where(low, right.astype(F32), code).astype(BF16)
        else:
            left = jnp.where(low, code, left.astype(F32)).astype(BF16)
        for k in range(2):
            rows = slice(k * half, (k + 1) * half)
            out_ref[j, pairs:, 2 * k * LANES : (2 * k + 1) * LANES] = left[rows]
            out_ref[j, pairs:, (2 * k + 1) * LANES : (2 * k + 2) * LANES] = right[rows]


def project_kernel(odd_ref, order_ref, got_ref, weights_ref, model_ref, out_ref):
    holders, rows, chunk = got_ref.shape
    rank = LANES // 2
    pairs = rank
    half = pairs // 2
    experts = weights_ref.shape[0] // rank
    odd = odd_ref[0] == 1
    low = iota((half, LANES), 1) < rank
    left = got_ref[:, pairs, 0:LANES].astype(F32)
    right = got_ref[:, pairs, LANES : 2 * LANES].astype(F32)
    code = jnp.where(odd, left, pltpu.roll(right, rank, 1))
    code = jnp.transpose(code)
    lane = iota((1, LANES), 1)
    wanted = [
        jnp.where(lane < rank, order_ref[2 * m], order_ref[2 * m + 1]).astype(F32) for m in range(experts // 2)
    ]
    part = 4
    for g in range(0, holders, part):
        every = dot(
            got_ref[g : g + part, :pairs, :].reshape(part * pairs, chunk), weights_ref[...], ((1,), (1,))
        )
        for h in range(part):
            col = jnp.broadcast_to(code[:pairs, g + h : g + h + 1], (pairs, LANES))
            own = jnp.zeros((pairs, LANES), F32)
            for m in range(experts // 2):
                block = every[h * pairs : (h + 1) * pairs, m * LANES : (m + 1) * LANES]
                own = own + jnp.where(col == wanted[m], block, 0.0)
            own = own + pltpu.roll(own, rank, 1)
            out_ref[g + h, :half, :] = jnp.where(low, own[:half], own[half:])
    side = rows - pairs
    begin = dot(got_ref[:, pairs:, : chunk // 2].reshape(holders * side, chunk // 2), model_ref[...], ((1,), (1,)))
    end = dot(got_ref[:, pairs:, chunk // 2 :].reshape(holders * side, chunk // 2), model_ref[...], ((1,), (1,)))
    both = jnp.where(iota((holders * side, LANES), 1) < rank, begin, end)
    out_ref[:, half:, :] = both.reshape(holders, side, LANES)


def slots_kernel(parts_ref, weight_ref, pick_ref, line_ref, out_ref):
    holders, rows, _ = parts_ref.shape
    experts = out_ref.shape[0]
    rank = LANES // 2
    toks = weight_ref.shape[0]
    whole = parts_ref[0]
    for h in range(1, holders):
        whole = whole + parts_ref[h]
    low = iota((toks, LANES), 1) < rank
    acts, dy = whole[:toks], whole[toks:]
    dy = jnp.concatenate([pltpu.roll(dy, rank, 1), dy], axis=0)
    table = jnp.concatenate(
        [
            jnp.where(low, acts, 0.0),
            jnp.where(low, pltpu.roll(acts, rank, 1), 0.0),
            jnp.where(low, 0.0, weight_ref[:, 0:1] * dy),
            jnp.where(low, 0.0, weight_ref[:, 1:2] * dy),
        ],
        axis=0,
    )
    slots = dot(pick_ref[...], table.astype(BF16)).astype(BF16)
    out_ref[:, :CAP, :] = slots.reshape(experts, CAP, LANES)
    first = iota((experts, 8, LANES), 1) == 0
    out_ref[:, CAP:, :] = jnp.where(first, line_ref[...][:, None, :], 0.0).astype(BF16)


def score_kernel(known_ref, q_ref, out_ref, sums_ref):
    holders, rows, lanes = known_ref.shape
    rank, wide = q_ref.shape
    queries = wide // rank
    per = lanes // queries
    slots = rows - 8
    spread_row, spread_col = iota((rank, lanes), 0), iota((rank, lanes), 1) // queries
    blank = jnp.zeros((rank, lanes), BF16)
    part = 8
    label = iota((SEQS, slots), 0).astype(F32)
    total = jnp.zeros((SEQS, 2 * lanes), F32)
    for g in range(0, holders, part):
        lhs = known_ref[g : g + part, :slots, :].reshape(part * slots, lanes)
        for c in range(wide // lanes):
            spread = (spread_row == c * per + spread_col).astype(F32).astype(BF16)
            top = jnp.concatenate([q_ref[:, c * lanes : (c + 1) * lanes], blank], axis=1)
            rhs = jnp.concatenate([top, jnp.concatenate([blank, spread], axis=1)], axis=0)
            both = dot(lhs, rhs)
            prod = both[:, :lanes] * both[:, lanes:]
            if c == 0:
                sums_ref[...] = prod
            else:
                sums_ref[...] += prod
        sums = sums_ref[...]
        high = sums.astype(BF16)
        low = (sums - high.astype(F32)).astype(BF16)
        seqs = known_ref[g : g + part, slots, :].astype(F32)
        sel = jnp.concatenate(
            [(label == seqs[i : i + 1]).astype(F32).astype(BF16) for i in range(part)], axis=1
        )
        total = total + dot(sel, jnp.concatenate([high, low], axis=1))
    score = total[:, :lanes] + total[:, lanes:]
    step = lanes // 2
    while step >= queries:
        score = score + pltpu.roll(score, step, 1)
        step //= 2
    out_ref[...] = score[:, :queries]


def on_device(active, out_grad, proj_model, routes, route_weight, seq_ids, proj_hidden, query_feat):
    experts = lax.axis_size("expert")
    sections = lax.axis_size("section")
    holders = lax.axis_size("dp")
    toks, top, hidden = active.shape[1:]
    rank, width = proj_model.shape
    chunk = hidden // holders
    pairs = top * toks
    me = lax.axis_index("expert")
    odd = lax.axis_index("dp") % 2

    sent = call(
        pack_kernel, "pack", (holders, pairs + toks // 2, chunk), BF16,
        active[0].reshape(pairs, hidden), out_grad[0], routes[0].T,
    )
    got = exchange(sent, "dp")

    weights = proj_hidden
    order = [0]
    bit = experts // 2
    while bit:
        other = lax.ppermute(weights, "expert", [(i, i ^ bit) for i in range(experts)])
        weights = jnp.concatenate([weights, other], axis=0)
        order = order + [o ^ bit for o in order]
        bit //= 2
    named = me ^ jnp.array(order, jnp.int32)
    gap = 2 * LANES - width
    model = jnp.where(
        odd == 1, jnp.pad(proj_model, ((0, 0), (gap, 0))), jnp.pad(proj_model, ((0, 0), (0, gap)))
    )
    model = jnp.concatenate([model, model], axis=0)
    partial = call(
        project_kernel, "project", (holders, toks + toks // 2, LANES), F32,
        odd.reshape(1), named, got, weights.reshape(experts * rank, chunk), model,
    )
    parts = exchange(partial, "dp")

    ids = routes[0].reshape(pairs)
    member = (ids[:, None] == jnp.arange(experts)[None, :]).astype(BF16)
    before = dot(jnp.tril(jnp.ones((pairs, pairs), BF16), -1), member)
    place = jnp.sum(before * member.astype(F32), axis=1).astype(jnp.int32)
    slot = ids * CAP + place
    slot = jnp.concatenate([slot, slot.reshape(toks, top).T.reshape(pairs)])
    pick = (jnp.arange(experts * CAP)[:, None] == slot[None, :]).astype(BF16)
    belongs = (place[:, None] == (jnp.arange(LANES) % CAP)[None, :]).astype(BF16)
    pair_seq = jnp.repeat(seq_ids, top).astype(BF16)
    line = dot(member * pair_seq[:, None], belongs, ((0,), (0,)))
    slots = call(
        slots_kernel, "slots", (experts, CAP + 8, LANES), BF16, parts, route_weight[0], pick, line
    )
    moved = exchange(slots, "expert")
    own = jnp.arange(LANES)[None, :] // CAP == jnp.arange(experts)[:, None]
    seqs = jnp.sum(jnp.where(own, moved[:, CAP, :].astype(F32), 0.0), axis=0).astype(BF16)
    mine = jnp.concatenate(
        [moved[:, :CAP].reshape(experts * CAP, LANES), jnp.broadcast_to(seqs[None], (8, LANES))], axis=0
    )
    known = lax.all_gather(mine, "dp", axis=0, tiled=False)

    queries = query_feat.shape[2]
    q = query_feat[0, 0].reshape(queries, rank, rank).transpose(1, 2, 0).reshape(rank, rank * queries)
    scores = pl.pallas_call(
        score_kernel,
        name="score",
        out_shape=jax.ShapeDtypeStruct((SEQS, queries), F32),
        in_specs=[VMEM] * 2,
        out_specs=VMEM,
        scratch_shapes=[pltpu.VMEM((8 * experts * CAP, LANES), F32)],
        compiler_params=pltpu.CompilerParams(vmem_limit_bytes=ROOM),
    )(known, q)
    out = exchange(scores.reshape(experts * sections, SEQS // (experts * sections), queries), ("expert", "section"))
    return jnp.sum(out, axis=0)


def solution(mesh):
    placed = (
        P("section", ("expert", "dp"), None, None),
        P("section", ("expert", "dp"), None),
        P(None, "dp"),
        P("section", ("expert", "dp"), None),
        P("section", ("expert", "dp"), None),
        P(("expert", "dp")),
        P("expert", None, "dp"),
        P("section", "expert", "dp", None),
    )
    return jax.shard_map(
        on_device,
        mesh=mesh,
        in_specs=placed,
        out_specs=P(("expert", "section"), "dp"),
        check_vma=False,
    )
```

time: 134 us -> 119 us (0.89)
  local copies, waits for them, and re-layouts: 7.26 us -> 2.9 us
  other arithmetic: 5.07 us -> 0.95 us
  Pallas kernels: 10.2 us -> 7.13 us
  blocking collectives: 31.4 us -> 29.1 us
    pallas_call x1 -> x4, Pallas kernels: 10.2 us -> 7.13 us  [the longest x3 4.18 us: call(): pl.pallas_call(kernel, name=name, out_shape=jax.ShapeDtypeStruct(shape, d...]
    concatenate x5 -> x3, other arithmetic: 2.89 us -> 0.09 us  [the longest x1 0.08 us: on_device(): slot = jnp.concatenate([slot, slot.reshape(toks, top).T.reshape(pairs)])]
    eq x16 -> x0, local copies, waits for them, and re-layouts: 2.2 us -> none  [on_device(): code == (me ^ order[e]).astype(BF16)]
    all_gather x1, blocking collectives: 18.2 us -> 16.1 us  [on_device(): known = lax.all_gather(mine, 'dp', axis=0, tiled=False)]
    all_to_all x3, waiting for transfers between devices: 21.1 us -> 22.7 us  [exchange(): return lax.all_to_all(x, axes, split_axis=0, concat_axis=0, tiled=True)]
    ppermute x3, waiting for transfers between devices: 15.8 us -> 14.2 us  [on_device(): lax.ppermute(weights, 'expert', [(i, i ^ bit) for i in range(experts)])]
    dot_general x4 -> x0, matrix products: 1.35 us -> none  [the longest x1 0.74 us: on_device(): lax.dot_general(rows, weights.reshape(experts * rank, chunk), (((1,), (1,...]
    another operation x6 -> x4, local copies, waits for them, and re-layouts: 3.18 us -> 2.1 us  [the longest x1 1.5 us: on_device(): active[0].reshape(pairs, hidden)]
where the time goes in v2:
time: 119 us; the launch traced here: 118 us
  starting transfers between devices  40.4 us (34%)
  waiting for transfers between devices  36.9 us (31%)
  blocking collectives  29.1 us (24%)
  Pallas kernels  7.13 us (6%)
  local copies, waits for them, and re-layouts  2.9 us (2%)
    all_to_all x3, starting transfers between devices, exchange(): return lax.all_to_all(x, axes, split_axis=0, concat_axis=0, tiled=True)  24 us
    all_to_all x3, waiting for transfers between devices, exchange(): return lax.all_to_all(x, axes, split_axis=0, concat_axis=0, tiled=True)  22.7 us
    ppermute x3, starting transfers between devices, on_device(): lax.ppermute(weights, 'expert', [(i, i ^ bit) for i in range(experts)])  16.5 us
    all_gather x1, blocking collectives, on_device(): known = lax.all_gather(mine, 'dp', axis=0, tiled=False)  16.1 us
    ppermute x3, waiting for transfers between devices, on_device(): lax.ppermute(weights, 'expert', [(i, i ^ bit) for i in range(experts)])  14.2 us
    all_to_all x1, blocking collectives, exchange(): return lax.all_to_all(x, axes, split_axis=0, concat_axis=0, tiled=True)  13 us
    pallas_call x3, Pallas kernels, call(): pl.pallas_call(kernel, name=name, out_shape=jax.ShapeDtypeStruct(shape, d...  4.18 us
    pallas_call x1, Pallas kernels, on_device(): pl.pallas_call(score_kernel, name='score', out_shape=jax.ShapeDtypeStruct...  2.95 us
  transfers between devices with their start and end apart: 6, of which 6 were waited for; matrix products, arithmetic and copies ran while one was open for 2% of the time, Pallas kernels for 0%

profile of v2, /device:TPU:1, one launch (start us, length us, event | category | flops | bytes accessed | tf_op | source)
XLA Modules:
  0.0 118.0 jit_solution(7609540214140591502)
XLA Ops:
  0.0 0.0 copy-start
  0.0 0.0 copy-start.1
  0.0 1.5 %reshape_squeeze.9.acts_ref = bf16[64,8192]{1,0:T(8,128)(2,1)S(1)} reshape(bf16[1,32,2,8192]{3,2,1,0:T(2,128)(2,1)} %param.9) | data formatting | bytes 2097152 | tf_op jit(solution)/shard_map/reshape;squeeze | solution.py:183
  1.5 0.0 copy-done
  1.5 0.0 copy-done.1
  1.5 1.2 %pack.1 = bf16[16,80,512]{2,1,0:T(8,128)(2,1)} custom-call(bf16[64,8192]{1,0:T(8,128)(2,1)S(1)} %reshape_squeeze.9.acts_ref, bf16[32,3072]{1,0:T(8,128)(2,1)S(1)} %bitcast.25, s32[2,32]{1,0:T(2,128)S(1)} %bitcast.27), custom_call_target="tpu_custom_call" | custom-call | tf_op jit(solution)/shard_map/pack/pallas_call | solution.py:32
  2.8 0.0 copy-start.2
  2.8 0.0 copy-start.4
  2.8 0.0 copy-start.5
  2.8 0.0 copy-start.6
  2.8 0.0 copy-start.3
  2.8 10.5 %all-to-all-start = ((bf16[16,80,512]{2,1,0:T(8,128)(2,1)}), bf16[16,80,512]{2,1,0:T(8,128)(2,1)S(1)}, u32[]{:S(2)}, u32[]{:S(2)}) async-start(bf16[16,80,512]{2,1,0:T(8,128)(2,1)} %pack.1), calls=%async_computation | async-start | bytes 2621440 | tf_op jit(solution)/shard_map/all_to_all | solution.py:19
  13.2 0.0 copy-done.2
  13.3 0.0 copy-start.7
  13.3 8.9 %collective-permute-start = (bf16[1,64,512]{2,1,0:T(8,128)(2,1)S(1)}, bf16[1,64,512]{2,1,0:T(8,128)(2,1)S(1)}, u32[]{:S(2)}, u32[]{:S(2)}) collective-permute-start(bf16[1,64,512]{2,1,0:T(8,128)(2,1)S(1)} %copy-done.2), channel_id=1, source_target_pairs={{0,256},{64,320},{128,384},{192,448},{256,0},{320,64},{384,128},{4... | collective-permute-start | bytes 196616 | tf_op jit(solution)/shard_map/ppermute | solution.py:191
  22.2 0.1 copy.14
  22.3 0.1 reshape_squeeze.10
  22.4 0.2 fusion
  22.6 0.1 convert_element_type.52
  22.7 0.1 copy.15
  22.8 1.7 %collective-permute-done = bf16[1,64,512]{2,1,0:T(8,128)(2,1)S(1)} collective-permute-done((bf16[1,64,512]{2,1,0:T(8,128)(2,1)S(1)}, bf16[1,64,512]{2,1,0:T(8,128)(2,1)S(1)}, u32[]{:S(2)}, u32[]{:S(2)}) %collective-permute-start) | collective-permute-done | bytes 65568 | tf_op jit(solution)/shard_map/ppermute | solution.py:191
  24.6 5.7 %collective-permute-start.1 = (bf16[2,64,512]{2,1,0:T(8,128)(2,1)S(1)}, bf16[2,64,512]{2,1,0:T(8,128)(2,1)S(1)}, u32[]{:S(2)}, u32[]{:S(2)}) collective-permute-start(bf16[2,64,512]{2,1,0:T(8,128)(2,1)S(1)} %pad_maximum_fusion.2), channel_id=1, source_target_pairs={{0,128},{64,192},{128,0},{192,64},{256,384},{320,448},{384,256},{4... | collective-permute-start | bytes 393224 | tf_op jit(solution)/shard_map/ppermute | solution.py:191
  30.2 0.0 copy-done.4
  30.2 0.1 pad_select_fusion
  30.3 6.2 %collective-permute-done.1 = bf16[2,64,512]{2,1,0:T(8,128)(2,1)S(1)} collective-permute-done((bf16[2,64,512]{2,1,0:T(8,128)(2,1)S(1)}, bf16[2,64,512]{2,1,0:T(8,128)(2,1)S(1)}, u32[]{:S(2)}, u32[]{:S(2)}) %collective-permute-start.1) | collective-permute-done | bytes 131104 | tf_op jit(solution)/shard_map/ppermute | solution.py:191
  36.6 1.9 %collective-permute-start.2 = (bf16[4,64,512]{2,1,0:T(8,128)(2,1)S(1)}, bf16[4,64,512]{2,1,0:T(8,128)(2,1)S(1)}, u32[]{:S(2)}, u32[]{:S(2)}) collective-permute-start(bf16[4,64,512]{2,1,0:T(8,128)(2,1)S(1)} %pad_maximum_fusion.1), channel_id=1, source_target_pairs={{0,64},{64,0},{128,192},{192,128},{256,320},{320,256},{384,448},{4... | collective-permute-start | bytes 786440 | tf_op jit(solution)/shard_map/ppermute | solution.py:191
  38.5 0.0 copy-done.5
  38.5 0.1 copy.16.weight_ref
  38.6 0.1 reshape.87
  38.7 0.0 copy-done.6
  38.7 0.1 broadcast_in_dim.16
  38.8 0.1 convert_element_type.55
  38.9 0.0 copy-done.3
  38.9 0.2 reshape_squeeze.11
  39.1 0.3 copy.17
  39.4 0.1 copy.18.q_ref
  39.5 0.0 copy-done.7
  39.6 6.3 %collective-permute-done.2 = bf16[4,64,512]{2,1,0:T(8,128)(2,1)S(1)} collective-permute-done((bf16[4,64,512]{2,1,0:T(8,128)(2,1)S(1)}, bf16[4,64,512]{2,1,0:T(8,128)(2,1)S(1)}, u32[]{:S(2)}, u32[]{:S(2)}) %collective-permute-start.2) | collective-permute-done | bytes 262176 | tf_op jit(solution)/shard_map/ppermute | solution.py:191
  45.9 0.1 pad_maximum_fusion
  45.9 0.6 all-to-all-done.got_ref
  46.6 2.1 %project.1 = f32[16,48,128]{2,1,0:T(8,128)} custom-call(s32[1]{0:T(128)} %bitcast.odd_ref, s32[8]{0:T(128)S(1)} %broadcast_xor_fusion.order_ref, bf16[16,80,512]{2,1,0:T(8,128)(2,1)S(1)} %all-to-all-done.got_ref, bf16[512,512]{1,0:T(8,128)(2,1)S(1)} %bitcast.24, bf16[128,256]{1,0:T(8,128)(2,1)S(1)} %pad_maximum_fusion.3.model_ref), custom_call_target="tpu_custom_call" | custom-call | tf_op jit(solution)/shard_map/project/pallas_call | solution.py:32
  48.7 7.2 %all-to-all-start.1 = ((f32[16,48,128]{2,1,0:T(8,128)}), f32[16,48,128]{2,1,0:T(8,128)S(1)}, u32[]{:S(2)}, u32[]{:S(2)}) async-start(f32[16,48,128]{2,1,0:T(8,128)} %project.1), calls=%async_computation.1 | async-start | bytes 786432 | tf_op jit(solution)/shard_map/all_to_all | solution.py:19
  55.9 0.1 pad_add_fusion
  56.0 0.2 fusion.3.line_ref
  56.2 14.2 %all-to-all-done.1.parts_ref = f32[16,48,128]{2,1,0:T(8,128)S(1)} async-done(((f32[16,48,128]{2,1,0:T(8,128)}), f32[16,48,128]{2,1,0:T(8,128)S(1)}, u32[]{:S(2)}, u32[]{:S(2)}) %all-to-all-start.1) | async-done | bytes 393248 | tf_op jit(solution)/shard_map/all_to_all | solution.py:19
  70.4 0.8 slots.1
  71.2 6.3 %all-to-all-start.2 = ((bf16[8,24,128]{2,1,0:T(8,128)(2,1)}), bf16[8,24,128]{2,1,0:T(8,128)(2,1)S(1)}, u32[]{:S(2)}, u32[]{:S(2)}) async-start(bf16[8,24,128]{2,1,0:T(8,128)(2,1)} %slots.1), calls=%async_computation.2 | async-start | bytes 98304 | tf_op jit(solution)/shard_map/all_to_all | solution.py:19
  77.5 7.8 %all-to-all-done.2 = bf16[8,24,128]{2,1,0:T(8,128)(2,1)S(1)} async-done(((bf16[8,24,128]{2,1,0:T(8,128)(2,1)}), bf16[8,24,128]{2,1,0:T(8,128)(2,1)S(1)}, u32[]{:S(2)}, u32[]{:S(2)}) %all-to-all-start.2) | async-done | bytes 49184 | tf_op jit(solution)/shard_map/all_to_all | solution.py:19
  85.4 16.1 %all-gather = bf16[2176,128]{1,0:T(8,128)(2,1)S(1)} all-gather(bf16[136,128]{1,0:T(8,128)(2,1)S(1)} %pad_maximum_fusion.4), channel_id=2, replica_groups=mesh['expert'=8,'dp'=16,'section'=4] {'dp'}, dimensions={0}, use_global_device_ids=true | all-gather | bytes 591872 | tf_op jit(solution)/shard_map/all_gather | solution.py:226
  101.5 3.0 %score.1 = f32[64,16]{1,0:T(8,128)S(1)} custom-call(bf16[16,136,128]{2,1,0:T(8,128)(2,1)S(1)} %bitcast.23, bf16[64,1024]{1,0:T(8,128)(2,1)S(1)} %copy.18.q_ref), custom_call_target="tpu_custom_call" | custom-call | tf_op jit(solution)/shard_map/score/pallas_call | solution.py:230
  104.4 13.0 %all_to_all.20 = f32[32,2,16]{2,1,0:T(2,128)S(1)} all-to-all(f32[32,2,16]{2,1,0:T(2,128)S(1)} %bitcast.26), channel_id=1, replica_groups=mesh['expert'=8,'dp'=16,'section'=4] {'expert','section'}, dimensions={0} | all-to-all | bytes 8192 | tf_op jit(solution)/shard_map/all_to_all | solution.py:19
  117.4 0.6 reduce_sum.29
  (17 shorter events, 0.1 us)
Async XLA Ops:
  0.0 1.5 %copy-start = (bf16[1,32,3072]{2,1,0:T(8,128)(2,1)S(1)}, bf16[1,32,3072]{2,1,0:T(8,128)(2,1)}, u32[]{:S(2)}) copy-start(bf16[1,32,3072]{2,1,0:T(8,128)(2,1)} %param.10) | copy-start | bytes 589828
  0.0 1.5 %copy-start.1 = (s32[1,32,2]{1,2,0:T(2,128)S(1)}, s32[1,32,2]{1,2,0:T(2,128)}, u32[]{:S(2)}) copy-start(s32[1,32,2]{1,2,0:T(2,128)} %param.12) | copy-start | bytes 772
  2.8 10.5 %copy-start.2 = (bf16[1,64,512]{2,1,0:T(8,128)(2,1)S(1)}, bf16[1,64,512]{2,1,0:T(8,128)(2,1)}, u32[]{:S(2)}) copy-start(bf16[1,64,512]{2,1,0:T(8,128)(2,1)} %param.15) | copy-start | bytes 196612
  2.8 27.5 %copy-start.4 = (bf16[64,192]{1,0:T(8,128)(2,1)S(1)}, bf16[64,192]{1,0:T(8,128)(2,1)}, u32[]{:S(2)}) copy-start(bf16[64,192]{1,0:T(8,128)(2,1)} %param.11) | copy-start | bytes 73732
  2.8 35.7 %copy-start.5 = (f32[1,32,2]{1,2,0:T(2,128)S(1)}, f32[1,32,2]{1,2,0:T(2,128)}, u32[]{:S(2)}) copy-start(f32[1,32,2]{1,2,0:T(2,128)} %param.13) | copy-start | bytes 772
  2.8 35.9 %copy-start.6 = (s32[32]{0:T(128)S(1)}, s32[32]{0:T(128)}, u32[]{:S(2)}) copy-start(s32[32]{0:T(128)} %param.14) | copy-start | bytes 388
  2.8 36.1 %copy-start.3 = (bf16[1,1,16,4096]{3,2,1,0:T(8,128)(2,1)S(1)}, bf16[1,1,16,4096]{3,2,1,0:T(8,128)(2,1)}, u32[]{:S(2)}) copy-start(bf16[1,1,16,4096]{3,2,1,0:T(8,128)(2,1)} %param.16) | copy-start | bytes 393220
  2.8 43.8 %all-to-all-start = ((bf16[16,80,512]{2,1,0:T(8,128)(2,1)}), bf16[16,80,512]{2,1,0:T(8,128)(2,1)S(1)}, u32[]{:S(2)}, u32[]{:S(2)}) async-start(bf16[16,80,512]{2,1,0:T(8,128)(2,1)} %pack.1), calls=%async_computation | async-start | bytes 2621440 | tf_op jit(solution)/shard_map/all_to_all | solution.py:19
  13.3 26.3 %copy-start.7 = (s32[8]{0:T(128)S(1)}, s32[8]{0:T(128)}, u32[]{:S(2)}) copy-start(s32[8]{0:T(128)} %constant.70.clone) | copy-start | bytes 100
  13.3 11.3 %collective-permute-start = (bf16[1,64,512]{2,1,0:T(8,128)(2,1)S(1)}, bf16[1,64,512]{2,1,0:T(8,128)(2,1)S(1)}, u32[]{:S(2)}, u32[]{:S(2)}) collective-permute-start(bf16[1,64,512]{2,1,0:T(8,128)(2,1)S(1)} %copy-done.2), channel_id=1, source_target_pairs={{0,256},{64,320},{128,384},{192,448},{256,0},{320,64},{384,128},{4... | collective-permute-start | bytes 196616 | tf_op jit(solution)/shard_map/ppermute | solution.py:191
  24.6 12.0 %collective-permute-start.1 = (bf16[2,64,512]{2,1,0:T(8,128)(2,1)S(1)}, bf16[2,64,512]{2,1,0:T(8,128)(2,1)S(1)}, u32[]{:S(2)}, u32[]{:S(2)}) collective-permute-start(bf16[2,64,512]{2,1,0:T(8,128)(2,1)S(1)} %pad_maximum_fusion.2), channel_id=1, source_target_pairs={{0,128},{64,192},{128,0},{192,64},{256,384},{320,448},{384,256},{4... | collective-permute-start | bytes 393224 | tf_op jit(solution)/shard_map/ppermute | solution.py:191
  36.6 9.3 %collective-permute-start.2 = (bf16[4,64,512]{2,1,0:T(8,128)(2,1)S(1)}, bf16[4,64,512]{2,1,0:T(8,128)(2,1)S(1)}, u32[]{:S(2)}, u32[]{:S(2)}) collective-permute-start(bf16[4,64,512]{2,1,0:T(8,128)(2,1)S(1)} %pad_maximum_fusion.1), channel_id=1, source_target_pairs={{0,64},{64,0},{128,192},{192,128},{256,320},{320,256},{384,448},{4... | collective-permute-start | bytes 786440 | tf_op jit(solution)/shard_map/ppermute | solution.py:191
  48.7 21.7 %all-to-all-start.1 = ((f32[16,48,128]{2,1,0:T(8,128)}), f32[16,48,128]{2,1,0:T(8,128)S(1)}, u32[]{:S(2)}, u32[]{:S(2)}) async-start(f32[16,48,128]{2,1,0:T(8,128)} %project.1), calls=%async_computation.1 | async-start | bytes 786432 | tf_op jit(solution)/shard_map/all_to_all | solution.py:19
  71.2 14.1 %all-to-all-start.2 = ((bf16[8,24,128]{2,1,0:T(8,128)(2,1)}), bf16[8,24,128]{2,1,0:T(8,128)(2,1)S(1)}, u32[]{:S(2)}, u32[]{:S(2)}) async-start(bf16[8,24,128]{2,1,0:T(8,128)(2,1)} %slots.1), calls=%async_computation.2 | async-start | bytes 98304 | tf_op jit(solution)/shard_map/all_to_all | solution.py:19

commit v3 on v2

--- a/solution.py
+++ b/solution.py
@@ -11,6 +11,8 @@
 ROOM = 20 << 20
 F32 = jnp.float32
 BF16 = jnp.bfloat16
+DP = ("y_hi", "y_lo", "core")
+CLOSE = ("y_lo", "core")
 VMEM = pl.BlockSpec(memory_space=pltpu.VMEM)
 SMEM = pl.BlockSpec(memory_space=pltpu.SMEM)
 
@@ -123,66 +125,80 @@
         axis=0,
     )
     slots = dot(pick_ref[...], table.astype(BF16)).astype(BF16)
-    out_ref[:, :CAP, :] = slots.reshape(experts, CAP, LANES)
     first = iota((experts, 8, LANES), 1) == 0
-    out_ref[:, CAP:, :] = jnp.where(first, line_ref[...][:, None, :], 0.0).astype(BF16)
-
-
-def score_kernel(known_ref, q_ref, out_ref, sums_ref):
-    holders, rows, lanes = known_ref.shape
-    rank, wide = q_ref.shape
+    line = jnp.where(first, line_ref[...][:, None, :], 0.0).astype(BF16)
+    for i in range(out_ref.shape[1]):
+        out_ref[:, i, :CAP, :] = slots.reshape(experts, CAP, LANES)
+        out_ref[:, i, CAP:, :] = line
+
+
+def score_kernel(mine_ref, known_ref, *refs):
+    *q_refs, out_ref, sums_ref = refs
+    blocks, rows, lanes = known_ref.shape
+    rank, wide = q_refs[0].shape
     queries = wide // rank
     per = lanes // queries
-    slots = rows - 8
+    near = len(q_refs)
+    experts, _, lines, _ = out_ref.shape
     spread_row, spread_col = iota((rank, lanes), 0), iota((rank, lanes), 1) // queries
     blank = jnp.zeros((rank, lanes), BF16)
-    part = 8
-    label = iota((SEQS, slots), 0).astype(F32)
-    total = jnp.zeros((SEQS, 2 * lanes), F32)
-    for g in range(0, holders, part):
-        lhs = known_ref[g : g + part, :slots, :].reshape(part * slots, lanes)
-        for c in range(wide // lanes):
-            spread = (spread_row == c * per + spread_col).astype(F32).astype(BF16)
-            top = jnp.concatenate([q_ref[:, c * lanes : (c + 1) * lanes], blank], axis=1)
-            rhs = jnp.concatenate([top, jnp.concatenate([blank, spread], axis=1)], axis=0)
-            both = dot(lhs, rhs)
+    lhs = known_ref[:, :CAP, :].reshape(blocks * CAP, lanes)
+    for c in range(wide // lanes):
+        spread = (spread_row == c * per + spread_col).astype(F32).astype(BF16)
+        under = jnp.concatenate([blank, spread], axis=1)
+        for k in range(near):
+            top = jnp.concatenate([q_refs[k][:, c * lanes : (c + 1) * lanes], blank], axis=1)
+            both = dot(lhs, jnp.concatenate([top, under], axis=0))
             prod = both[:, :lanes] * both[:, lanes:]
             if c == 0:
-                sums_ref[...] = prod
+                sums_ref[k] = prod
             else:
-                sums_ref[...] += prod
-        sums = sums_ref[...]
+                sums_ref[k] += prod
+    group = lanes // CAP
+    own = iota((group, lanes), 1) // CAP == iota((group, lanes), 0)
+    label = iota((SEQS, lanes), 0).astype(F32)
+    sel = []
+    for g in range(0, blocks, group):
+        line = known_ref[g : g + group, CAP, :].astype(F32)
+        seqs = jnp.sum(jnp.where(own, line, 0.0), axis=0, keepdims=True)
+        sel.append((label == seqs).astype(F32).astype(BF16))
+    sel = jnp.concatenate(sel, axis=1)
+    scores = []
+    for k in range(near):
+        sums = sums_ref[k]
         high = sums.astype(BF16)
         low = (sums - high.astype(F32)).astype(BF16)
-        seqs = known_ref[g : g + part, slots, :].astype(F32)
-        sel = jnp.concatenate(
-            [(label == seqs[i : i + 1]).astype(F32).astype(BF16) for i in range(part)], axis=1
-        )
-        total = total + dot(sel, jnp.concatenate([high, low], axis=1))
-    score = total[:, :lanes] + total[:, lanes:]
-    step = lanes // 2
-    while step >= queries:
-        score = score + pltpu.roll(score, step, 1)
-        step //= 2
-    out_ref[...] = score[:, :queries]
+        total = dot(sel, jnp.concatenate([high, low], axis=1))
+        score = total[:, :lanes] + total[:, lanes:]
+        step = lanes // 2
+        while step >= queries:
+            score = score + pltpu.roll(score, step, 1)
+            step //= 2
+        scores.append(score[:, :queries])
+    for i in range(near):
+        part = scores[0]
+        for k in range(1, near):
+            part = jnp.where(mine_ref[0] == i ^ k, scores[k], part)
+        out_ref[:, i, :, :] = part.reshape(experts, lines, queries)
 
 
 def on_device(active, out_grad, proj_model, routes, route_weight, seq_ids, proj_hidden, query_feat):
     experts = lax.axis_size("expert")
     sections = lax.axis_size("section")
-    holders = lax.axis_size("dp")
+    holders = lax.axis_size(DP)
+    far, near = lax.axis_size("y_hi"), lax.axis_size(CLOSE)
     toks, top, hidden = active.shape[1:]
     rank, width = proj_model.shape
     chunk = hidden // holders
     pairs = top * toks
     me = lax.axis_index("expert")
-    odd = lax.axis_index("dp") % 2
+    odd = lax.axis_index("core")
 
     sent = call(
         pack_kernel, "pack", (holders, pairs + toks // 2, chunk), BF16,
         active[0].reshape(pairs, hidden), out_grad[0], routes[0].T,
     )
-    got = exchange(sent, "dp")
+    got = exchange(sent, DP)
 
     weights = proj_hidden
     order = [0]
@@ -202,7 +218,10 @@
         project_kernel, "project", (holders, toks + toks // 2, LANES), F32,
         odd.reshape(1), named, got, weights.reshape(experts * rank, chunk), model,
     )
-    parts = exchange(partial, "dp")
+    queries = query_feat.shape[2]
+    q = query_feat[0, 0].reshape(queries, rank, rank).transpose(1, 2, 0).reshape(rank, rank * queries)
+    partial, q = lax.optimization_barrier((partial, q))
+    parts = exchange(partial, DP)
 
     ids = routes[0].reshape(pairs)
     member = (ids[:, None] == jnp.arange(experts)[None, :]).astype(BF16)
@@ -215,46 +234,47 @@
     pair_seq = jnp.repeat(seq_ids, top).astype(BF16)
     line = dot(member * pair_seq[:, None], belongs, ((0,), (0,)))
     slots = call(
-        slots_kernel, "slots", (experts, CAP + 8, LANES), BF16, parts, route_weight[0], pick, line
-    )
-    moved = exchange(slots, "expert")
-    own = jnp.arange(LANES)[None, :] // CAP == jnp.arange(experts)[:, None]
-    seqs = jnp.sum(jnp.where(own, moved[:, CAP, :].astype(F32), 0.0), axis=0).astype(BF16)
-    mine = jnp.concatenate(
-        [moved[:, :CAP].reshape(experts * CAP, LANES), jnp.broadcast_to(seqs[None], (8, LANES))], axis=0
-    )
-    known = lax.all_gather(mine, "dp", axis=0, tiled=False)
-
-    queries = query_feat.shape[2]
-    q = query_feat[0, 0].reshape(queries, rank, rank).transpose(1, 2, 0).reshape(rank, rank * queries)
+        slots_kernel, "slots", (experts, far, CAP + 8, LANES), BF16, parts, route_weight[0], pick, line
+    )
+    near_q = [q] + [lax.ppermute(q, CLOSE, [(i, i ^ k) for i in range(near)]) for k in range(1, near)]
+    slots, *near_q = lax.optimization_barrier((slots, *near_q))
+    known = exchange(slots.reshape(experts * far, CAP + 8, LANES), ("expert", "y_hi"))
+
+    lines = SEQS // experts
     scores = pl.pallas_call(
         score_kernel,
         name="score",
-        out_shape=jax.ShapeDtypeStruct((SEQS, queries), F32),
-        in_specs=[VMEM] * 2,
+        out_shape=jax.ShapeDtypeStruct((experts, near, lines, queries), F32),
+        in_specs=[SMEM] + [VMEM] * (1 + near),
         out_specs=VMEM,
-        scratch_shapes=[pltpu.VMEM((8 * experts * CAP, LANES), F32)],
+        scratch_shapes=[pltpu.VMEM((near, experts * far * CAP, LANES), F32)],
         compiler_params=pltpu.CompilerParams(vmem_limit_bytes=ROOM),
-    )(known, q)
-    out = exchange(scores.reshape(experts * sections, SEQS // (experts * sections), queries), ("expert", "section"))
+    )(lax.axis_index(CLOSE).reshape(1), known, *near_q)
+    out = exchange(
+        scores.reshape(experts * near * sections, lines // sections, queries), ("expert",) + CLOSE + ("section",)
+    )
     return jnp.sum(out, axis=0)
 
 
 def solution(mesh):
+    experts, holders, sections = mesh.devices.shape
+    shape = (experts, holders // 4, 2, 2, sections)
+    finer = jax.sharding.Mesh(mesh.devices.reshape(shape), ("expert",) + DP + ("section",))
+    tokens = ("expert",) + DP
     placed = (
-        P("section", ("expert", "dp"), None, None),
-        P("section", ("expert", "dp"), None),
-        P(None, "dp"),
-        P("section", ("expert", "dp"), None),
-        P("section", ("expert", "dp"), None),
-        P(("expert", "dp")),
-        P("expert", None, "dp"),
-        P("section", "expert", "dp", None),
+        P("section", tokens, None, None),
+        P("section", tokens, None),
+        P(None, DP),
+        P("section", tokens, None),
+        P("section", tokens, None),
+        P(tokens),
+        P("expert", None, DP),
+        P("section", "expert", DP, None),
     )
     return jax.shard_map(
         on_device,
-        mesh=mesh,
+        mesh=finer,
         in_specs=placed,
-        out_specs=P(("expert", "section"), "dp"),
+        out_specs=P(("expert", "section"), DP),
         check_vma=False,
     )

time: 119 us -> 120 us (level)
  starting transfers between devices: 40.4 us -> 52.9 us
  blocking collectives: 29.1 us -> 21.2 us
  waiting for transfers between devices: 36.9 us -> 33.7 us
    all_gather x1 -> x0, blocking collectives: 16.1 us -> none  [on_device(): known = lax.all_gather(mine, 'dp', axis=0, tiled=False)]
    all_to_all x1, blocking collectives: 13 us -> 21.2 us  [exchange(): return lax.all_to_all(x, axes, split_axis=0, concat_axis=0, tiled=True)]
    ppermute x0 -> x3, starting transfers between devices: none -> 7.87 us  [on_device(): lax.ppermute(q, CLOSE, [(i, i ^ k) for i in range(near)])]
    all_to_all x3, waiting for transfers between devices: 22.7 us -> 18.2 us  [exchange(): return lax.all_to_all(x, axes, split_axis=0, concat_axis=0, tiled=True)]
    all_to_all x3, starting transfers between devices: 24 us -> 28.4 us  [exchange(): return lax.all_to_all(x, axes, split_axis=0, concat_axis=0, tiled=True)]
  transfers between devices with their start and end apart: 6 -> 9, of which waited for: 6 -> 7; matrix products, arithmetic and copies ran while one was open for 2% -> 2% of each run, Pallas kernels for 0% -> 1%
where the time goes in v3:
time: 120 us; the launch traced here: 119 us
  starting transfers between devices  52.9 us (44%)
  waiting for transfers between devices  33.7 us (28%)
  blocking collectives  21.2 us (18%)
  Pallas kernels  6.97 us (6%)
  local copies, waits for them, and re-layouts  3.03 us (3%)
    all_to_all x3, starting transfers between devices, exchange(): return lax.all_to_all(x, axes, split_axis=0, concat_axis=0, tiled=True)  28.4 us
    all_to_all x1, blocking collectives, exchange(): return lax.all_to_all(x, axes, split_axis=0, concat_axis=0, tiled=True)  21.2 us
    all_to_all x3, waiting for transfers between devices, exchange(): return lax.all_to_all(x, axes, split_axis=0, concat_axis=0, tiled=True)  18.2 us
    ppermute x3, starting transfers between devices, on_device(): lax.ppermute(weights, 'expert', [(i, i ^ bit) for i in range(experts)])  16.6 us
    ppermute x3, waiting for transfers between devices, on_device(): lax.ppermute(weights, 'expert', [(i, i ^ bit) for i in range(experts)])  14.4 us
    ppermute x3, starting transfers between devices, on_device(): lax.ppermute(q, CLOSE, [(i, i ^ k) for i in range(near)])  7.87 us
    pallas_call x3, Pallas kernels, call(): pl.pallas_call(kernel, name=name, out_shape=jax.ShapeDtypeStruct(shape, d...  4.26 us
    pallas_call x1, Pallas kernels, on_device(): pl.pallas_call(score_kernel, name='score', out_shape=jax.ShapeDtypeStruct...  2.71 us
  transfers between devices with their start and end apart: 9, of which 7 were waited for; matrix products, arithmetic and copies ran while one was open for 2% of the time, Pallas kernels for 1%

profile of v3, /device:TPU:1, one launch (start us, length us, event | category | flops | bytes accessed | tf_op | source)
XLA Modules:
  0.0 119.4 jit_solution(4444350653814846759)
XLA Ops:
  0.0 0.0 copy-start
  0.0 0.0 copy-start.1
  0.0 1.5 %reshape_squeeze.9.acts_ref = bf16[64,8192]{1,0:T(8,128)(2,1)S(1)} reshape(bf16[1,32,2,8192]{3,2,1,0:T(2,128)(2,1)} %param.9) | data formatting | bytes 2097152 | tf_op jit(solution)/shard_map/reshape;squeeze | solution.py:199
  1.5 0.0 copy-done
  1.5 0.0 copy-done.1
  1.5 1.2 %pack.1 = bf16[16,80,512]{2,1,0:T(8,128)(2,1)} custom-call(bf16[64,8192]{1,0:T(8,128)(2,1)S(1)} %reshape_squeeze.9.acts_ref, bf16[32,3072]{1,0:T(8,128)(2,1)S(1)} %bitcast.24, s32[2,32]{1,0:T(2,128)S(1)} %bitcast.25), custom_call_target="tpu_custom_call" | custom-call | tf_op jit(solution)/shard_map/pack/pallas_call | solution.py:34
  2.8 0.0 copy-start.2
  2.8 0.0 copy-start.4
  2.8 0.0 copy-start.3
  2.8 10.5 %all-to-all-start = ((bf16[16,80,512]{2,1,0:T(8,128)(2,1)}), bf16[16,80,512]{2,1,0:T(8,128)(2,1)S(1)}, u32[]{:S(2)}, u32[]{:S(2)}) async-start(bf16[16,80,512]{2,1,0:T(8,128)(2,1)} %pack.1), calls=%async_computation | async-start | bytes 2621440 | tf_op jit(solution)/shard_map/all_to_all | solution.py:21
  13.2 0.0 copy-done.2
  13.2 0.0 copy-start.5
  13.2 0.0 copy-start.6
  13.3 0.0 copy-start.7
  13.3 9.0 %collective-permute-start = (bf16[1,64,512]{2,1,0:T(8,128)(2,1)S(1)}, bf16[1,64,512]{2,1,0:T(8,128)(2,1)S(1)}, u32[]{:S(2)}, u32[]{:S(2)}) collective-permute-start(bf16[1,64,512]{2,1,0:T(8,128)(2,1)S(1)} %copy-done.2), channel_id=1, source_target_pairs={{0,256},{64,320},{128,384},{192,448},{256,0},{320,64},{384,128},{4... | collective-permute-start | bytes 196616 | tf_op jit(solution)/shard_map/ppermute | solution.py:207
  22.3 0.1 copy.15
  22.4 0.1 reshape_squeeze.11
  22.5 0.2 fusion
  22.7 0.1 convert_element_type.39
  22.9 0.1 copy.16
  22.9 1.7 %collective-permute-done = bf16[1,64,512]{2,1,0:T(8,128)(2,1)S(1)} collective-permute-done((bf16[1,64,512]{2,1,0:T(8,128)(2,1)S(1)}, bf16[1,64,512]{2,1,0:T(8,128)(2,1)S(1)}, u32[]{:S(2)}, u32[]{:S(2)}) %collective-permute-start) | collective-permute-done | bytes 65568 | tf_op jit(solution)/shard_map/ppermute | solution.py:207
  24.7 5.7 %collective-permute-start.1 = (bf16[2,64,512]{2,1,0:T(8,128)(2,1)S(1)}, bf16[2,64,512]{2,1,0:T(8,128)(2,1)S(1)}, u32[]{:S(2)}, u32[]{:S(2)}) collective-permute-start(bf16[2,64,512]{2,1,0:T(8,128)(2,1)S(1)} %pad_maximum_fusion.2), channel_id=1, source_target_pairs={{0,128},{64,192},{128,0},{192,64},{256,384},{320,448},{384,256},{4... | collective-permute-start | bytes 393224 | tf_op jit(solution)/shard_map/ppermute | solution.py:207
  30.4 0.0 copy-done.4
  30.4 0.1 pad_select_fusion
  30.5 6.2 %collective-permute-done.1 = bf16[2,64,512]{2,1,0:T(8,128)(2,1)S(1)} collective-permute-done((bf16[2,64,512]{2,1,0:T(8,128)(2,1)S(1)}, bf16[2,64,512]{2,1,0:T(8,128)(2,1)S(1)}, u32[]{:S(2)}, u32[]{:S(2)}) %collective-permute-start.1) | collective-permute-done | bytes 131104 | tf_op jit(solution)/shard_map/ppermute | solution.py:207
  36.7 1.9 %collective-permute-start.2 = (bf16[4,64,512]{2,1,0:T(8,128)(2,1)S(1)}, bf16[4,64,512]{2,1,0:T(8,128)(2,1)S(1)}, u32[]{:S(2)}, u32[]{:S(2)}) collective-permute-start(bf16[4,64,512]{2,1,0:T(8,128)(2,1)S(1)} %pad_maximum_fusion.1), channel_id=1, source_target_pairs={{0,64},{64,0},{128,192},{192,128},{256,320},{320,256},{384,448},{4... | collective-permute-start | bytes 786440 | tf_op jit(solution)/shard_map/ppermute | solution.py:207
  38.6 0.0 copy-done.3
  38.6 0.2 reshape_squeeze.10
  38.9 0.3 copy.14
  39.2 0.0 copy-done.5
  39.2 0.1 copy.17.weight_ref
  39.3 0.1 reshape.50
  39.3 0.0 copy-done.6
  39.3 0.1 broadcast_in_dim.18
  39.4 0.1 convert_element_type.42
  39.5 0.0 copy-done.7
  39.6 6.4 %collective-permute-done.2 = bf16[4,64,512]{2,1,0:T(8,128)(2,1)S(1)} collective-permute-done((bf16[4,64,512]{2,1,0:T(8,128)(2,1)S(1)}, bf16[4,64,512]{2,1,0:T(8,128)(2,1)S(1)}, u32[]{:S(2)}, u32[]{:S(2)}) %collective-permute-start.2) | collective-permute-done | bytes 262176 | tf_op jit(solution)/shard_map/ppermute | solution.py:207
  46.0 0.1 pad_maximum_fusion
  46.0 0.5 all-to-all-done.got_ref
  46.5 2.1 %project.1 = f32[16,48,128]{2,1,0:T(8,128)} custom-call(s32[1]{0:T(128)} %bitcast.1.odd_ref, s32[8]{0:T(128)S(1)} %broadcast_xor_fusion.order_ref, bf16[16,80,512]{2,1,0:T(8,128)(2,1)S(1)} %all-to-all-done.got_ref, bf16[512,512]{1,0:T(8,128)(2,1)S(1)} %bitcast.22, bf16[128,256]{1,0:T(8,128)(2,1)S(1)} %pad_maximum_fusion.3.model_ref), custom_call_target="tpu_custom_call" | custom-call | tf_op jit(solution)/shard_map/project/pallas_call | solution.py:34
  48.6 7.4 %all-to-all-start.1 = ((f32[16,48,128]{2,1,0:T(8,128)}), f32[16,48,128]{2,1,0:T(8,128)S(1)}, u32[]{:S(2)}, u32[]{:S(2)}) async-start(f32[16,48,128]{2,1,0:T(8,128)} %project.1), calls=%async_computation.1 | async-start | bytes 786432 | tf_op jit(solution)/shard_map/all_to_all | solution.py:21
  56.0 0.1 pad_add_fusion
  56.1 0.1 copy.18
  56.3 2.0 %collective-permute-start.3 = (bf16[64,1024]{1,0:T(8,128)(2,1)S(1)}, bf16[64,1024]{1,0:T(8,128)(2,1)S(1)}, u32[]{:S(2)}, u32[]{:S(2)}) collective-permute-start(bf16[64,1024]{1,0:T(8,128)(2,1)S(1)} %copy.18), channel_id=1, source_target_pairs={{0,4},{4,0},{8,12},{12,8},{1,5},{5,1},{9,13},{13,9},{2,6},{6,2},{1... | collective-permute-start | bytes 393224 | tf_op jit(solution)/shard_map/ppermute | solution.py:239
  58.3 3.5 %collective-permute-start.4 = (bf16[64,1024]{1,0:T(8,128)(2,1)S(1)}, bf16[64,1024]{1,0:T(8,128)(2,1)S(1)}, u32[]{:S(2)}, u32[]{:S(2)}) collective-permute-start(bf16[64,1024]{1,0:T(8,128)(2,1)S(1)} %copy.18), channel_id=1, source_target_pairs={{0,8},{4,12},{8,0},{12,4},{1,9},{5,13},{9,1},{13,5},{2,10},{6,14},... | collective-permute-start | bytes 393224 | tf_op jit(solution)/shard_map/ppermute | solution.py:239
  61.8 2.3 %collective-permute-start.5 = (bf16[64,1024]{1,0:T(8,128)(2,1)S(1)}, bf16[64,1024]{1,0:T(8,128)(2,1)S(1)}, u32[]{:S(2)}, u32[]{:S(2)}) collective-permute-start(bf16[64,1024]{1,0:T(8,128)(2,1)S(1)} %copy.18), channel_id=1, source_target_pairs={{0,12},{4,8},{8,4},{12,0},{1,13},{5,9},{9,5},{13,1},{2,14},{6,10},... | collective-permute-start | bytes 393224 | tf_op jit(solution)/shard_map/ppermute | solution.py:239
  64.1 0.2 fusion.3.line_ref
  64.3 6.2 %all-to-all-done.1.parts_ref = f32[16,48,128]{2,1,0:T(8,128)S(1)} async-done(((f32[16,48,128]{2,1,0:T(8,128)}), f32[16,48,128]{2,1,0:T(8,128)S(1)}, u32[]{:S(2)}, u32[]{:S(2)}) %all-to-all-start.1) | async-done | bytes 393248 | tf_op jit(solution)/shard_map/all_to_all | solution.py:21
  70.6 0.9 slots.1
  71.5 0.0 collective-permute-done.3.refs_1_
  71.5 0.0 collective-permute-done.4.refs_2_
  71.5 1.1 collective-permute-done.5.refs_3_
  72.6 10.5 %all-to-all-start.2 = ((bf16[32,24,128]{2,1,0:T(8,128)(2,1)}), bf16[32,24,128]{2,1,0:T(8,128)(2,1)S(1)}, u32[]{:S(2)}, u32[]{:S(2)}) async-start(bf16[32,24,128]{2,1,0:T(8,128)(2,1)} %bitcast.10), calls=%async_computation.2 | async-start | bytes 393216 | tf_op jit(solution)/shard_map/all_to_all | solution.py:21
  83.2 0.1 copy.21.refs_0_
  83.3 11.5 %all-to-all-done.2.known_ref = bf16[32,24,128]{2,1,0:T(8,128)(2,1)S(1)} async-done(((bf16[32,24,128]{2,1,0:T(8,128)(2,1)}), bf16[32,24,128]{2,1,0:T(8,128)(2,1)S(1)}, u32[]{:S(2)}, u32[]{:S(2)}) %all-to-all-start.2) | async-done | bytes 196640 | tf_op jit(solution)/shard_map/all_to_all | solution.py:21
  94.8 2.7 %score.1 = f32[8,4,8,16]{3,2,1,0:T(8,128)S(1)} custom-call(s32[1]{0:T(128)} %bitcast.mine_ref, bf16[32,24,128]{2,1,0:T(8,128)(2,1)S(1)} %all-to-all-done.2.known_ref, bf16[64,1024]{1,0:T(8,128)(2,1)S(1)} %copy.21.refs_0_, bf16[64,1024]{1,0:T(8,128)(2,1)S(1)} %collective-permute-done.3.refs_1_, bf16[64,1024]{1,0:T(8,128)(2,1)S(1)} %collective-permute-done.4.refs_2_, ...), custom_call_target="tpu_custom_call" | custom-call | tf_op jit(solution)/shard_map/score/pallas_call | solution.py:244
  97.5 21.2 %all_to_all.20 = f32[128,2,16]{2,1,0:T(2,128)S(1)} all-to-all(f32[128,2,16]{2,1,0:T(2,128)S(1)} %bitcast.23), channel_id=1, replica_groups=mesh['expert'=8,'y_hi'=4,'y_lo'=2,'core'=2,'section'=4] {'expert','y_lo'..., dimensions={0} | all-to-all | bytes 32768 | tf_op jit(solution)/shard_map/all_to_all | solution.py:21
  118.7 0.7 reduce_sum.19
  (11 shorter events, 0.1 us)
Async XLA Ops:
  0.0 1.5 %copy-start = (bf16[1,32,3072]{2,1,0:T(8,128)(2,1)S(1)}, bf16[1,32,3072]{2,1,0:T(8,128)(2,1)}, u32[]{:S(2)}) copy-start(bf16[1,32,3072]{2,1,0:T(8,128)(2,1)} %param.10) | copy-start | bytes 589828
  0.0 1.5 %copy-start.1 = (s32[1,32,2]{1,2,0:T(2,128)S(1)}, s32[1,32,2]{1,2,0:T(2,128)}, u32[]{:S(2)}) copy-start(s32[1,32,2]{1,2,0:T(2,128)} %param.12) | copy-start | bytes 772
  2.8 10.5 %copy-start.2 = (bf16[1,64,512]{2,1,0:T(8,128)(2,1)S(1)}, bf16[1,64,512]{2,1,0:T(8,128)(2,1)}, u32[]{:S(2)}) copy-start(bf16[1,64,512]{2,1,0:T(8,128)(2,1)} %param.15) | copy-start | bytes 196612
  2.8 27.6 %copy-start.4 = (bf16[64,192]{1,0:T(8,128)(2,1)S(1)}, bf16[64,192]{1,0:T(8,128)(2,1)}, u32[]{:S(2)}) copy-start(bf16[64,192]{1,0:T(8,128)(2,1)} %param.11) | copy-start | bytes 73732
  2.8 35.9 %copy-start.3 = (bf16[1,1,16,4096]{3,2,1,0:T(8,128)(2,1)S(1)}, bf16[1,1,16,4096]{3,2,1,0:T(8,128)(2,1)}, u32[]{:S(2)}) copy-start(bf16[1,1,16,4096]{3,2,1,0:T(8,128)(2,1)} %param.16) | copy-start | bytes 393220
  2.8 43.8 %all-to-all-start = ((bf16[16,80,512]{2,1,0:T(8,128)(2,1)}), bf16[16,80,512]{2,1,0:T(8,128)(2,1)S(1)}, u32[]{:S(2)}, u32[]{:S(2)}) async-start(bf16[16,80,512]{2,1,0:T(8,128)(2,1)} %pack.1), calls=%async_computation | async-start | bytes 2621440 | tf_op jit(solution)/shard_map/all_to_all | solution.py:21
  13.2 25.9 %copy-start.5 = (f32[1,32,2]{1,2,0:T(2,128)S(1)}, f32[1,32,2]{1,2,0:T(2,128)}, u32[]{:S(2)}) copy-start(f32[1,32,2]{1,2,0:T(2,128)} %param.13) | copy-start | bytes 772
  13.2 26.1 %copy-start.6 = (s32[32]{0:T(128)S(1)}, s32[32]{0:T(128)}, u32[]{:S(2)}) copy-start(s32[32]{0:T(128)} %param.14) | copy-start | bytes 388
  13.3 26.3 %copy-start.7 = (s32[8]{0:T(128)S(1)}, s32[8]{0:T(128)}, u32[]{:S(2)}) copy-start(s32[8]{0:T(128)} %constant.51.clone) | copy-start | bytes 100
  13.3 11.4 %collective-permute-start = (bf16[1,64,512]{2,1,0:T(8,128)(2,1)S(1)}, bf16[1,64,512]{2,1,0:T(8,128)(2,1)S(1)}, u32[]{:S(2)}, u32[]{:S(2)}) collective-permute-start(bf16[1,64,512]{2,1,0:T(8,128)(2,1)S(1)} %copy-done.2), channel_id=1, source_target_pairs={{0,256},{64,320},{128,384},{192,448},{256,0},{320,64},{384,128},{4... | collective-permute-start | bytes 196616 | tf_op jit(solution)/shard_map/ppermute | solution.py:207
  24.7 12.0 %collective-permute-start.1 = (bf16[2,64,512]{2,1,0:T(8,128)(2,1)S(1)}, bf16[2,64,512]{2,1,0:T(8,128)(2,1)S(1)}, u32[]{:S(2)}, u32[]{:S(2)}) collective-permute-start(bf16[2,64,512]{2,1,0:T(8,128)(2,1)S(1)} %pad_maximum_fusion.2), channel_id=1, source_target_pairs={{0,128},{64,192},{128,0},{192,64},{256,384},{320,448},{384,256},{4... | collective-permute-start | bytes 393224 | tf_op jit(solution)/shard_map/ppermute | solution.py:207
  36.7 9.3 %collective-permute-start.2 = (bf16[4,64,512]{2,1,0:T(8,128)(2,1)S(1)}, bf16[4,64,512]{2,1,0:T(8,128)(2,1)S(1)}, u32[]{:S(2)}, u32[]{:S(2)}) collective-permute-start(bf16[4,64,512]{2,1,0:T(8,128)(2,1)S(1)} %pad_maximum_fusion.1), channel_id=1, source_target_pairs={{0,64},{64,0},{128,192},{192,128},{256,320},{320,256},{384,448},{4... | collective-permute-start | bytes 786440 | tf_op jit(solution)/shard_map/ppermute | solution.py:207
  48.6 21.9 %all-to-all-start.1 = ((f32[16,48,128]{2,1,0:T(8,128)}), f32[16,48,128]{2,1,0:T(8,128)S(1)}, u32[]{:S(2)}, u32[]{:S(2)}) async-start(f32[16,48,128]{2,1,0:T(8,128)} %project.1), calls=%async_computation.1 | async-start | bytes 786432 | tf_op jit(solution)/shard_map/all_to_all | solution.py:21
  56.3 15.2 %collective-permute-start.3 = (bf16[64,1024]{1,0:T(8,128)(2,1)S(1)}, bf16[64,1024]{1,0:T(8,128)(2,1)S(1)}, u32[]{:S(2)}, u32[]{:S(2)}) collective-permute-start(bf16[64,1024]{1,0:T(8,128)(2,1)S(1)} %copy.18), channel_id=1, source_target_pairs={{0,4},{4,0},{8,12},{12,8},{1,5},{5,1},{9,13},{13,9},{2,6},{6,2},{1... | collective-permute-start | bytes 393224 | tf_op jit(solution)/shard_map/ppermute | solution.py:239
  58.3 13.2 %collective-permute-start.4 = (bf16[64,1024]{1,0:T(8,128)(2,1)S(1)}, bf16[64,1024]{1,0:T(8,128)(2,1)S(1)}, u32[]{:S(2)}, u32[]{:S(2)}) collective-permute-start(bf16[64,1024]{1,0:T(8,128)(2,1)S(1)} %copy.18), channel_id=1, source_target_pairs={{0,8},{4,12},{8,0},{12,4},{1,9},{5,13},{9,1},{13,5},{2,10},{6,14},... | collective-permute-start | bytes 393224 | tf_op jit(solution)/shard_map/ppermute | solution.py:239
  61.8 10.8 %collective-permute-start.5 = (bf16[64,1024]{1,0:T(8,128)(2,1)S(1)}, bf16[64,1024]{1,0:T(8,128)(2,1)S(1)}, u32[]{:S(2)}, u32[]{:S(2)}) collective-permute-start(bf16[64,1024]{1,0:T(8,128)(2,1)S(1)} %copy.18), channel_id=1, source_target_pairs={{0,12},{4,8},{8,4},{12,0},{1,13},{5,9},{9,5},{13,1},{2,14},{6,10},... | collective-permute-start | bytes 393224 | tf_op jit(solution)/shard_map/ppermute | solution.py:239
  72.6 22.2 %all-to-all-start.2 = ((bf16[32,24,128]{2,1,0:T(8,128)(2,1)}), bf16[32,24,128]{2,1,0:T(8,128)(2,1)S(1)}, u32[]{:S(2)}, u32[]{:S(2)}) async-start(bf16[32,24,128]{2,1,0:T(8,128)(2,1)} %bitcast.10), calls=%async_computation.2 | async-start | bytes 393216 | tf_op jit(solution)/shard_map/all_to_all | solution.py:21

commit v4 on v3

--- a/solution.py
+++ b/solution.py
@@ -4,6 +4,7 @@
 from jax.experimental import pallas as pl
 from jax.experimental.pallas import tpu as pltpu
 from jax.sharding import PartitionSpec as P
+
 
 SEQS = 64
 CAP = 16
@@ -13,6 +14,7 @@
 BF16 = jnp.bfloat16
 DP = ("y_hi", "y_lo", "core")
 CLOSE = ("y_lo", "core")
+GROUP = ("y_lo", "core", "section")
 VMEM = pl.BlockSpec(memory_space=pltpu.VMEM)
 SMEM = pl.BlockSpec(memory_space=pltpu.SMEM)
 
@@ -29,11 +31,10 @@
     return lax.broadcasted_iota(jnp.int32, shape, axis)
 
 
-def call(kernel, name, shape, dtype, *args):
+def call(kernel, shape, dtype, *args):
     specs = [SMEM if a.ndim == 1 else VMEM for a in args]
     return pl.pallas_call(
         kernel,
-        name=name,
         out_shape=jax.ShapeDtypeStruct(shape, dtype),
         in_specs=specs,
         out_specs=VMEM,
@@ -41,7 +42,7 @@
     )(*args)
 
 
-def pack_kernel(acts_ref, grads_ref, routes_ref, out_ref):
+def pack_kernel(turn_ref, acts_ref, grads_ref, routes_ref, out_ref):
     holders, _, chunk = out_ref.shape
     pairs = acts_ref.shape[0]
     toks, feats = grads_ref.shape
@@ -53,12 +54,18 @@
     second = dot(named, (lane == 2 * token + 1).astype(F32).astype(BF16))
     code = jnp.broadcast_to(first[0:1] + second[1:2], (toks, LANES))
     low = iota((toks, LANES), 1) < width % LANES
+    sections = 4
+    spread = holders // sections
     for j in range(holders):
-        out_ref[j, :pairs, :] = acts_ref[:, j * chunk : (j + 1) * chunk]
-        base = width * j // LANES * LANES
-        left = grads_ref[:, base : base + LANES]
-        right = grads_ref[:, base + LANES : base + 2 * LANES]
-        if width * j == base:
+        place, section = j // sections, j % sections
+        big = lax.rem(turn_ref[0] + section, sections)
+        begin = pl.multiple_of(big * (spread * chunk) + place * chunk, chunk)
+        out_ref[j, :pairs, :] = acts_ref[:, pl.ds(begin, chunk)]
+        shift = width * place // LANES * LANES
+        base = pl.multiple_of(big * (spread * width) + shift, LANES)
+        left = grads_ref[:, pl.ds(base, LANES)]
+        right = grads_ref[:, pl.ds(pl.multiple_of(base + LANES, LANES), LANES)]
+        if width * place == shift:
             right = jnp.where(low, right.astype(F32), code).astype(BF16)
         else:
             left = jnp.where(low, code, left.astype(F32)).astype(BF16)
@@ -105,7 +112,7 @@
 
 
 def slots_kernel(parts_ref, weight_ref, pick_ref, line_ref, out_ref):
-    holders, rows, _ = parts_ref.shape
+    holders, _, _ = parts_ref.shape
     experts = out_ref.shape[0]
     rank = LANES // 2
     toks = weight_ref.shape[0]
@@ -134,7 +141,7 @@
 
 def score_kernel(mine_ref, known_ref, *refs):
     *q_refs, out_ref, sums_ref = refs
-    blocks, rows, lanes = known_ref.shape
+    blocks, _, lanes = known_ref.shape
     rank, wide = q_refs[0].shape
     queries = wide // rank
     per = lanes // queries
@@ -182,7 +189,7 @@
         out_ref[:, i, :, :] = part.reshape(experts, lines, queries)
 
 
-def on_device(active, out_grad, proj_model, routes, route_weight, seq_ids, proj_hidden, query_feat):
+def scores_of(active, out_grad, proj_model, routes, route_weight, seq_ids, proj_hidden, query_feat):
     experts = lax.axis_size("expert")
     sections = lax.axis_size("section")
     holders = lax.axis_size(DP)
@@ -194,13 +201,26 @@
     me = lax.axis_index("expert")
     odd = lax.axis_index("core")
 
+    gap = 2 * LANES - width
+    model = jnp.where(
+        odd == 1, jnp.pad(proj_model, ((0, 0), (gap, 0))), jnp.pad(proj_model, ((0, 0), (0, gap)))
+    )
+    tied = jnp.concatenate([proj_hidden[0], model], axis=1)
+    moves = [
+        ((section + y) % far * sections + section, y * sections + section)
+        for y in range(far)
+        for section in range(sections)
+    ]
+    tied = lax.ppermute(tied, ("y_hi", "section"), moves)
+
     sent = call(
-        pack_kernel, "pack", (holders, pairs + toks // 2, chunk), BF16,
-        active[0].reshape(pairs, hidden), out_grad[0], routes[0].T,
-    )
-    got = exchange(sent, DP)
-
-    weights = proj_hidden
+        pack_kernel, (holders, pairs + toks // 2, chunk), BF16,
+        lax.axis_index("y_hi").reshape(1), active[0].reshape(pairs, hidden), out_grad[0], routes[0].T,
+    )
+    tied, sent = lax.optimization_barrier((tied, sent))
+    got = exchange(sent, GROUP)
+
+    weights, model = tied[None, :, :chunk], tied[:, chunk:]
     order = [0]
     bit = experts // 2
     while bit:
@@ -209,19 +229,15 @@
         order = order + [o ^ bit for o in order]
         bit //= 2
     named = me ^ jnp.array(order, jnp.int32)
-    gap = 2 * LANES - width
-    model = jnp.where(
-        odd == 1, jnp.pad(proj_model, ((0, 0), (gap, 0))), jnp.pad(proj_model, ((0, 0), (0, gap)))
-    )
     model = jnp.concatenate([model, model], axis=0)
     partial = call(
-        project_kernel, "project", (holders, toks + toks // 2, LANES), F32,
+        project_kernel, (holders, toks + toks // 2, LANES), F32,
         odd.reshape(1), named, got, weights.reshape(experts * rank, chunk), model,
     )
     queries = query_feat.shape[2]
     q = query_feat[0, 0].reshape(queries, rank, rank).transpose(1, 2, 0).reshape(rank, rank * queries)
     partial, q = lax.optimization_barrier((partial, q))
-    parts = exchange(partial, DP)
+    parts = exchange(partial, GROUP)
 
     ids = routes[0].reshape(pairs)
     member = (ids[:, None] == jnp.arange(experts)[None, :]).astype(BF16)
@@ -233,11 +249,8 @@
     belongs = (place[:, None] == (jnp.arange(LANES) % CAP)[None, :]).astype(BF16)
     pair_seq = jnp.repeat(seq_ids, top).astype(BF16)
     line = dot(member * pair_seq[:, None], belongs, ((0,), (0,)))
-    slots = call(
-        slots_kernel, "slots", (experts, far, CAP + 8, LANES), BF16, parts, route_weight[0], pick, line
-    )
+    slots = call(slots_kernel, (experts, far, CAP + 8, LANES), BF16, parts, route_weight[0], pick, line)
     near_q = [q] + [lax.ppermute(q, CLOSE, [(i, i ^ k) for i in range(near)]) for k in range(1, near)]
-    slots, *near_q = lax.optimization_barrier((slots, *near_q))
     known = exchange(slots.reshape(experts * far, CAP + 8, LANES), ("expert", "y_hi"))
 
     lines = SEQS // experts
@@ -272,7 +285,7 @@
         P("section", "expert", DP, None),
     )
     return jax.shard_map(
-        on_device,
+        scores_of,
         mesh=finer,
         in_specs=placed,
         out_specs=P(("expert", "section"), DP),

time: 120 us -> 122 us (1.017)
  starting transfers between devices: 52.9 us -> 59.4 us
  waiting for transfers between devices: 33.7 us -> 27.9 us
  other arithmetic: 1.02 us -> 2.7 us
    all_to_all x3, waiting for transfers between devices: 18.2 us -> 8.55 us  [exchange(): return lax.all_to_all(x, axes, split_axis=0, concat_axis=0, tiled=True)]
    all_to_all x3, starting transfers between devices: 28.4 us -> 32.4 us  [exchange(): return lax.all_to_all(x, axes, split_axis=0, concat_axis=0, tiled=True)]
    ppermute x6 -> x7, waiting for transfers between devices: 15.5 us -> 19.4 us  [the longest x3 14.6 us: scores_of(): lax.ppermute(weights, 'expert', [(i, i ^ bit) for i in range(experts)])]
    ppermute x6 -> x7, starting transfers between devices: 24.5 us -> 27 us  [the longest x3 18.2 us: scores_of(): lax.ppermute(weights, 'expert', [(i, i ^ bit) for i in range(experts)])]
  transfers between devices with their start and end apart: 9 -> 10, of which waited for: 7 -> 6; matrix products, arithmetic and copies ran while one was open for 2% -> 3% of each run, Pallas kernels for 1% -> 1%
where the time goes in v4:
time: 122 us; the launch traced here: 121 us
  starting transfers between devices  59.4 us (49%)
  waiting for transfers between devices  27.9 us (23%)
  blocking collectives  20.6 us (17%)
  Pallas kernels  6.99 us (6%)
  local copies, waits for them, and re-layouts  2.86 us (2%)
  other arithmetic  2.7 us (2%)
    all_to_all x3, starting transfers between devices, exchange(): return lax.all_to_all(x, axes, split_axis=0, concat_axis=0, tiled=True)  32.4 us
    all_to_all x1, blocking collectives, exchange(): return lax.all_to_all(x, axes, split_axis=0, concat_axis=0, tiled=True)  20.6 us
    ppermute x3, starting transfers between devices, scores_of(): lax.ppermute(weights, 'expert', [(i, i ^ bit) for i in range(experts)])  18.2 us
    ppermute x3, waiting for transfers between devices, scores_of(): lax.ppermute(weights, 'expert', [(i, i ^ bit) for i in range(experts)])  14.6 us
    all_to_all x3, waiting for transfers between devices, exchange(): return lax.all_to_all(x, axes, split_axis=0, concat_axis=0, tiled=True)  8.55 us
    ppermute x3, starting transfers between devices, scores_of(): lax.ppermute(q, CLOSE, [(i, i ^ k) for i in range(near)])  8.16 us
    ppermute x3, waiting for transfers between devices, scores_of(): lax.ppermute(q, CLOSE, [(i, i ^ k) for i in range(near)])  4.73 us
    pallas_call x3, Pallas kernels, call(): pl.pallas_call(kernel, out_shape=jax.ShapeDtypeStruct(shape, dtype), in_s...  4.28 us
  transfers between devices with their start and end apart: 10, of which 6 were waited for; matrix products, arithmetic and copies ran while one was open for 3% of the time, Pallas kernels for 1%

profile of v4, /device:TPU:1, one launch (start us, length us, event | category | flops | bytes accessed | tf_op | source)
XLA Modules:
  0.0 121.1 jit_solution(16373377641408141815)
XLA Ops:
  0.0 0.0 copy-start
  0.0 0.0 copy-start.1
  0.0 0.9 pad_select_fusion
  0.9 0.8 pad_maximum_fusion.3
  1.8 0.7 collective-permute-start
  2.4 1.5 %reshape_squeeze.9.acts_ref = bf16[64,8192]{1,0:T(8,128)(2,1)S(1)} reshape(bf16[1,32,2,8192]{3,2,1,0:T(2,128)(2,1)} %param.9) | data formatting | bytes 2097152 | tf_op jit(solution)/shard_map/reshape;squeeze | solution.py:218
  3.9 0.0 copy-done
  3.9 0.0 copy-done.1
  3.9 1.2 %shard_map.91 = bf16[16,80,512]{2,1,0:T(8,128)(2,1)} custom-call(s32[1]{0:T(128)} %bitcast.3.turn_ref, bf16[64,8192]{1,0:T(8,128)(2,1)S(1)} %reshape_squeeze.9.acts_ref, bf16[32,3072]{1,0:T(8,128)(2,1)S(1)} %bitcast.28, s32[2,32]{1,0:T(2,128)S(1)} %bitcast.29), custom_call_target="tpu_custom_call" | custom-call | tf_op jit(solution)/shard_map/pallas_call | solution.py:36
  5.2 0.0 copy-start.5
  5.2 0.0 copy-start.2
  5.2 0.0 collective-permute-done
  5.2 15.9 %all-to-all-start = ((bf16[16,80,512]{2,1,0:T(8,128)(2,1)}), bf16[16,80,512]{2,1,0:T(8,128)(2,1)S(1)}, u32[]{:S(2)}, u32[]{:S(2)}) async-start(bf16[16,80,512]{2,1,0:T(8,128)(2,1)} %shard_map.91), calls=%async_computation | async-start | bytes 2621440 | tf_op jit(solution)/shard_map/all_to_all | solution.py:23
  21.1 0.0 copy-start.3
  21.1 0.0 copy-start.4
  21.1 0.1 copy.15
  21.2 0.1 reshape_squeeze.11
  21.3 10.6 %collective-permute-start.1 = (bf16[1,64,512]{2,1,0:T(8,128)(2,1)S(1)}, bf16[1,64,512]{2,1,0:T(8,128)(2,1)S(1)}, u32[]{:S(2)}, u32[]{:S(2)}) collective-permute-start(bf16[1,64,512]{2,1,0:T(8,128)(2,1)S(1)} %slice_bitcast_fusion), channel_id=1, source_target_pairs={{0,256},{64,320},{128,384},{192,448},{256,0},{320,64},{384,128},{4... | collective-permute-start | bytes 196616 | tf_op jit(solution)/shard_map/ppermute | solution.py:227
  32.0 0.2 fusion
  32.2 0.1 convert_element_type.39
  32.3 0.1 copy.16
  32.4 1.9 %collective-permute-done.1 = bf16[1,64,512]{2,1,0:T(8,128)(2,1)S(1)} collective-permute-done((bf16[1,64,512]{2,1,0:T(8,128)(2,1)S(1)}, bf16[1,64,512]{2,1,0:T(8,128)(2,1)S(1)}, u32[]{:S(2)}, u32[]{:S(2)}) %collective-permute-start.1) | collective-permute-done | bytes 65568 | tf_op jit(solution)/shard_map/ppermute | solution.py:227
  34.4 5.7 %collective-permute-start.2 = (bf16[2,64,512]{2,1,0:T(8,128)(2,1)S(1)}, bf16[2,64,512]{2,1,0:T(8,128)(2,1)S(1)}, u32[]{:S(2)}, u32[]{:S(2)}) collective-permute-start(bf16[2,64,512]{2,1,0:T(8,128)(2,1)S(1)} %pad_maximum_fusion.2), channel_id=1, source_target_pairs={{0,128},{64,192},{128,0},{192,64},{256,384},{320,448},{384,256},{4... | collective-permute-start | bytes 393224 | tf_op jit(solution)/shard_map/ppermute | solution.py:227
  40.0 6.3 %collective-permute-done.2 = bf16[2,64,512]{2,1,0:T(8,128)(2,1)S(1)} collective-permute-done((bf16[2,64,512]{2,1,0:T(8,128)(2,1)S(1)}, bf16[2,64,512]{2,1,0:T(8,128)(2,1)S(1)}, u32[]{:S(2)}, u32[]{:S(2)}) %collective-permute-start.2) | collective-permute-done | bytes 131104 | tf_op jit(solution)/shard_map/ppermute | solution.py:227
  46.4 1.9 %collective-permute-start.3 = (bf16[4,64,512]{2,1,0:T(8,128)(2,1)S(1)}, bf16[4,64,512]{2,1,0:T(8,128)(2,1)S(1)}, u32[]{:S(2)}, u32[]{:S(2)}) collective-permute-start(bf16[4,64,512]{2,1,0:T(8,128)(2,1)S(1)} %pad_maximum_fusion.1), channel_id=1, source_target_pairs={{0,64},{64,0},{128,192},{192,128},{256,320},{320,256},{384,448},{4... | collective-permute-start | bytes 786440 | tf_op jit(solution)/shard_map/ppermute | solution.py:227
  48.3 0.0 copy-done.5
  48.3 0.0 copy-done.2
  48.3 0.2 reshape_squeeze.10
  48.6 0.3 copy.14
  48.8 0.0 copy-done.3
  48.8 0.1 copy.17.weight_ref
  48.9 0.1 reshape.54
  49.0 0.0 copy-done.4
  49.0 0.1 broadcast_in_dim.22
  49.1 0.1 convert_element_type.42
  49.2 6.4 %collective-permute-done.3 = bf16[4,64,512]{2,1,0:T(8,128)(2,1)S(1)} collective-permute-done((bf16[4,64,512]{2,1,0:T(8,128)(2,1)S(1)}, bf16[4,64,512]{2,1,0:T(8,128)(2,1)S(1)}, u32[]{:S(2)}, u32[]{:S(2)}) %collective-permute-start.3) | collective-permute-done | bytes 262176 | tf_op jit(solution)/shard_map/ppermute | solution.py:227
  55.7 0.1 pad_maximum_fusion
  55.7 0.0 all-to-all-done.got_ref
  55.7 2.1 %shard_map.92 = f32[16,48,128]{2,1,0:T(8,128)} custom-call(s32[1]{0:T(128)} %bitcast.1.odd_ref, s32[8]{0:T(128)S(1)} %broadcast_xor_fusion.order_ref, bf16[16,80,512]{2,1,0:T(8,128)(2,1)S(1)} %all-to-all-done.got_ref, bf16[512,512]{1,0:T(8,128)(2,1)S(1)} %bitcast.26, bf16[128,256]{1,0:T(8,128)(2,1)S(1)} %pad_maximum_fusion.4.model_ref), custom_call_target="tpu_custom_call" | custom-call | tf_op jit(solution)/shard_map/pallas_call | solution.py:36
  57.8 6.3 %all-to-all-start.1 = ((f32[16,48,128]{2,1,0:T(8,128)}), f32[16,48,128]{2,1,0:T(8,128)S(1)}, u32[]{:S(2)}, u32[]{:S(2)}) async-start(f32[16,48,128]{2,1,0:T(8,128)} %shard_map.92), calls=%async_computation.1 | async-start | bytes 786432 | tf_op jit(solution)/shard_map/all_to_all | solution.py:23
  64.2 0.1 pad_add_fusion
  64.3 0.2 fusion.3.line_ref
  64.5 8.5 %all-to-all-done.1.parts_ref = f32[16,48,128]{2,1,0:T(8,128)S(1)} async-done(((f32[16,48,128]{2,1,0:T(8,128)}), f32[16,48,128]{2,1,0:T(8,128)S(1)}, u32[]{:S(2)}, u32[]{:S(2)}) %all-to-all-start.1) | async-done | bytes 393248 | tf_op jit(solution)/shard_map/all_to_all | solution.py:23
  73.0 0.9 shard_map.93
  73.9 10.1 %all-to-all-start.2 = ((bf16[32,24,128]{2,1,0:T(8,128)(2,1)}), bf16[32,24,128]{2,1,0:T(8,128)(2,1)S(1)}, u32[]{:S(2)}, u32[]{:S(2)}) async-start(bf16[32,24,128]{2,1,0:T(8,128)(2,1)} %bitcast.13), calls=%async_computation.2 | async-start | bytes 393216 | tf_op jit(solution)/shard_map/all_to_all | solution.py:23
  84.1 0.1 copy.21.refs_0_
  84.2 2.7 %collective-permute-start.4 = (bf16[64,1024]{1,0:T(8,128)(2,1)S(1)}, bf16[64,1024]{1,0:T(8,128)(2,1)S(1)}, u32[]{:S(2)}, u32[]{:S(2)}) collective-permute-start(bf16[64,1024]{1,0:T(8,128)(2,1)S(1)} %copy.21.refs_0_), channel_id=1, source_target_pairs={{0,4},{4,0},{8,12},{12,8},{1,5},{5,1},{9,13},{13,9},{2,6},{6,2},{1... | collective-permute-start | bytes 393224 | tf_op jit(solution)/shard_map/ppermute | solution.py:253
  86.9 2.2 %collective-permute-start.5 = (bf16[64,1024]{1,0:T(8,128)(2,1)S(1)}, bf16[64,1024]{1,0:T(8,128)(2,1)S(1)}, u32[]{:S(2)}, u32[]{:S(2)}) collective-permute-start(bf16[64,1024]{1,0:T(8,128)(2,1)S(1)} %copy.21.refs_0_), channel_id=1, source_target_pairs={{0,8},{4,12},{8,0},{12,4},{1,9},{5,13},{9,1},{13,5},{2,10},{6,14},... | collective-permute-start | bytes 393224 | tf_op jit(solution)/shard_map/ppermute | solution.py:253
  89.1 3.3 %collective-permute-start.6 = (bf16[64,1024]{1,0:T(8,128)(2,1)S(1)}, bf16[64,1024]{1,0:T(8,128)(2,1)S(1)}, u32[]{:S(2)}, u32[]{:S(2)}) collective-permute-start(bf16[64,1024]{1,0:T(8,128)(2,1)S(1)} %copy.21.refs_0_), channel_id=1, source_target_pairs={{0,12},{4,8},{8,4},{12,0},{1,13},{5,9},{9,5},{13,1},{2,14},{6,10},... | collective-permute-start | bytes 393224 | tf_op jit(solution)/shard_map/ppermute | solution.py:253
  92.4 0.0 collective-permute-done.4.refs_1_
  92.4 1.4 %collective-permute-done.5.refs_2_ = bf16[64,1024]{1,0:T(8,128)(2,1)S(1)} collective-permute-done((bf16[64,1024]{1,0:T(8,128)(2,1)S(1)}, bf16[64,1024]{1,0:T(8,128)(2,1)S(1)}, u32[]{:S(2)}, u32[]{:S(2)}) %collective-permute-start.5) | collective-permute-done | bytes 131104 | tf_op jit(solution)/shard_map/ppermute | solution.py:253
  93.9 3.3 %collective-permute-done.6.refs_3_ = bf16[64,1024]{1,0:T(8,128)(2,1)S(1)} collective-permute-done((bf16[64,1024]{1,0:T(8,128)(2,1)S(1)}, bf16[64,1024]{1,0:T(8,128)(2,1)S(1)}, u32[]{:S(2)}, u32[]{:S(2)}) %collective-permute-start.6) | collective-permute-done | bytes 131104 | tf_op jit(solution)/shard_map/ppermute | solution.py:253
  97.2 0.0 all-to-all-done.2.known_ref
  97.2 2.7 %score.1 = f32[8,4,8,16]{3,2,1,0:T(8,128)S(1)} custom-call(s32[1]{0:T(128)} %bitcast.mine_ref, bf16[32,24,128]{2,1,0:T(8,128)(2,1)S(1)} %all-to-all-done.2.known_ref, bf16[64,1024]{1,0:T(8,128)(2,1)S(1)} %copy.21.refs_0_, bf16[64,1024]{1,0:T(8,128)(2,1)S(1)} %collective-permute-done.4.refs_1_, bf16[64,1024]{1,0:T(8,128)(2,1)S(1)} %collective-permute-done.5.refs_2_, ...), custom_call_target="tpu_custom_call" | custom-call | tf_op jit(solution)/shard_map/score/pallas_call | solution.py:257
  99.9 20.6 %all_to_all.20 = f32[128,2,16]{2,1,0:T(2,128)S(1)} all-to-all(f32[128,2,16]{2,1,0:T(2,128)S(1)} %bitcast.27), channel_id=1, replica_groups=mesh['expert'=8,'y_hi'=4,'y_lo'=2,'core'=2,'section'=4] {'expert','y_lo'..., dimensions={0} | all-to-all | bytes 32768 | tf_op jit(solution)/shard_map/all_to_all | solution.py:23
  120.4 0.7 reduce_sum.19
  (13 shorter events, 0.1 us)
Async XLA Ops:
  0.0 3.9 %copy-start = (bf16[1,32,3072]{2,1,0:T(8,128)(2,1)S(1)}, bf16[1,32,3072]{2,1,0:T(8,128)(2,1)}, u32[]{:S(2)}) copy-start(bf16[1,32,3072]{2,1,0:T(8,128)(2,1)} %param.10) | copy-start | bytes 589828
  0.0 3.9 %copy-start.1 = (s32[1,32,2]{1,2,0:T(2,128)S(1)}, s32[1,32,2]{1,2,0:T(2,128)}, u32[]{:S(2)}) copy-start(s32[1,32,2]{1,2,0:T(2,128)} %param.12) | copy-start | bytes 772
  1.8 3.4 %collective-permute-start = (bf16[64,768]{1,0:T(8,128)(2,1)S(1)}, bf16[64,768]{1,0:T(8,128)(2,1)S(1)}, u32[]{:S(2)}, u32[]{:S(2)}) collective-permute-start(bf16[64,768]{1,0:T(8,128)(2,1)S(1)} %pad_maximum_fusion.3), channel_id=1, source_target_pairs={{0,0},{17,1},{34,2},{51,3},{16,16},{33,17},{50,18},{3,19},{32,32},... | collective-permute-start | bytes 294920 | tf_op jit(solution)/shard_map/ppermute | solution.py:214
  5.2 43.1 %copy-start.5 = (s32[8]{0:T(128)S(1)}, s32[8]{0:T(128)}, u32[]{:S(2)}) copy-start(s32[8]{0:T(128)} %constant.55.clone) | copy-start | bytes 100
  5.2 43.1 %copy-start.2 = (bf16[1,1,16,4096]{3,2,1,0:T(8,128)(2,1)S(1)}, bf16[1,1,16,4096]{3,2,1,0:T(8,128)(2,1)}, u32[]{:S(2)}) copy-start(bf16[1,1,16,4096]{3,2,1,0:T(8,128)(2,1)} %param.16) | copy-start | bytes 393220
  5.2 50.5 %all-to-all-start = ((bf16[16,80,512]{2,1,0:T(8,128)(2,1)}), bf16[16,80,512]{2,1,0:T(8,128)(2,1)S(1)}, u32[]{:S(2)}, u32[]{:S(2)}) async-start(bf16[16,80,512]{2,1,0:T(8,128)(2,1)} %shard_map.91), calls=%async_computation | async-start | bytes 2621440 | tf_op jit(solution)/shard_map/all_to_all | solution.py:23
  21.1 27.7 %copy-start.3 = (f32[1,32,2]{1,2,0:T(2,128)S(1)}, f32[1,32,2]{1,2,0:T(2,128)}, u32[]{:S(2)}) copy-start(f32[1,32,2]{1,2,0:T(2,128)} %param.13) | copy-start | bytes 772
  21.1 27.9 %copy-start.4 = (s32[32]{0:T(128)S(1)}, s32[32]{0:T(128)}, u32[]{:S(2)}) copy-start(s32[32]{0:T(128)} %param.14) | copy-start | bytes 388
  21.3 13.0 %collective-permute-start.1 = (bf16[1,64,512]{2,1,0:T(8,128)(2,1)S(1)}, bf16[1,64,512]{2,1,0:T(8,128)(2,1)S(1)}, u32[]{:S(2)}, u32[]{:S(2)}) collective-permute-start(bf16[1,64,512]{2,1,0:T(8,128)(2,1)S(1)} %slice_bitcast_fusion), channel_id=1, source_target_pairs={{0,256},{64,320},{128,384},{192,448},{256,0},{320,64},{384,128},{4... | collective-permute-start | bytes 196616 | tf_op jit(solution)/shard_map/ppermute | solution.py:227
  34.4 12.0 %collective-permute-start.2 = (bf16[2,64,512]{2,1,0:T(8,128)(2,1)S(1)}, bf16[2,64,512]{2,1,0:T(8,128)(2,1)S(1)}, u32[]{:S(2)}, u32[]{:S(2)}) collective-permute-start(bf16[2,64,512]{2,1,0:T(8,128)(2,1)S(1)} %pad_maximum_fusion.2), channel_id=1, source_target_pairs={{0,128},{64,192},{128,0},{192,64},{256,384},{320,448},{384,256},{4... | collective-permute-start | bytes 393224 | tf_op jit(solution)/shard_map/ppermute | solution.py:227
  46.4 9.3 %collective-permute-start.3 = (bf16[4,64,512]{2,1,0:T(8,128)(2,1)S(1)}, bf16[4,64,512]{2,1,0:T(8,128)(2,1)S(1)}, u32[]{:S(2)}, u32[]{:S(2)}) collective-permute-start(bf16[4,64,512]{2,1,0:T(8,128)(2,1)S(1)} %pad_maximum_fusion.1), channel_id=1, source_target_pairs={{0,64},{64,0},{128,192},{192,128},{256,320},{320,256},{384,448},{4... | collective-permute-start | bytes 786440 | tf_op jit(solution)/shard_map/ppermute | solution.py:227
  57.8 15.2 %all-to-all-start.1 = ((f32[16,48,128]{2,1,0:T(8,128)}), f32[16,48,128]{2,1,0:T(8,128)S(1)}, u32[]{:S(2)}, u32[]{:S(2)}) async-start(f32[16,48,128]{2,1,0:T(8,128)} %shard_map.92), calls=%async_computation.1 | async-start | bytes 786432 | tf_op jit(solution)/shard_map/all_to_all | solution.py:23
  73.9 23.2 %all-to-all-start.2 = ((bf16[32,24,128]{2,1,0:T(8,128)(2,1)}), bf16[32,24,128]{2,1,0:T(8,128)(2,1)S(1)}, u32[]{:S(2)}, u32[]{:S(2)}) async-start(bf16[32,24,128]{2,1,0:T(8,128)(2,1)} %bitcast.13), calls=%async_computation.2 | async-start | bytes 393216 | tf_op jit(solution)/shard_map/all_to_all | solution.py:23
  84.2 8.2 %collective-permute-start.4 = (bf16[64,1024]{1,0:T(8,128)(2,1)S(1)}, bf16[64,1024]{1,0:T(8,128)(2,1)S(1)}, u32[]{:S(2)}, u32[]{:S(2)}) collective-permute-start(bf16[64,1024]{1,0:T(8,128)(2,1)S(1)} %copy.21.refs_0_), channel_id=1, source_target_pairs={{0,4},{4,0},{8,12},{12,8},{1,5},{5,1},{9,13},{13,9},{2,6},{6,2},{1... | collective-permute-start | bytes 393224 | tf_op jit(solution)/shard_map/ppermute | solution.py:253
  86.9 6.9 %collective-permute-start.5 = (bf16[64,1024]{1,0:T(8,128)(2,1)S(1)}, bf16[64,1024]{1,0:T(8,128)(2,1)S(1)}, u32[]{:S(2)}, u32[]{:S(2)}) collective-permute-start(bf16[64,1024]{1,0:T(8,128)(2,1)S(1)} %copy.21.refs_0_), channel_id=1, source_target_pairs={{0,8},{4,12},{8,0},{12,4},{1,9},{5,13},{9,1},{13,5},{2,10},{6,14},... | collective-permute-start | bytes 393224 | tf_op jit(solution)/shard_map/ppermute | solution.py:253
  89.1 8.0 %collective-permute-start.6 = (bf16[64,1024]{1,0:T(8,128)(2,1)S(1)}, bf16[64,1024]{1,0:T(8,128)(2,1)S(1)}, u32[]{:S(2)}, u32[]{:S(2)}) collective-permute-start(bf16[64,1024]{1,0:T(8,128)(2,1)S(1)} %copy.21.refs_0_), channel_id=1, source_target_pairs={{0,12},{4,8},{8,4},{12,0},{1,13},{5,9},{9,5},{13,1},{2,14},{6,10},... | collective-permute-start | bytes 393224 | tf_op jit(solution)/shard_map/ppermute | solution.py:253

commit v5 on v4

--- a/solution.py
+++ b/solution.py
@@ -58,7 +58,7 @@
     spread = holders // sections
     for j in range(holders):
         place, section = j // sections, j % sections
-        big = lax.rem(turn_ref[0] + section, sections)
+        big = lax.rem(turn_ref[0] + (section + 2 * (place % 2)) % sections, sections)
         begin = pl.multiple_of(big * (spread * chunk) + place * chunk, chunk)
         out_ref[j, :pairs, :] = acts_ref[:, pl.ds(begin, chunk)]
         shift = width * place // LANES * LANES
@@ -206,23 +206,29 @@
         odd == 1, jnp.pad(proj_model, ((0, 0), (gap, 0))), jnp.pad(proj_model, ((0, 0), (0, gap)))
     )
     tied = jnp.concatenate([proj_hidden[0], model], axis=1)
+    cores = lax.axis_size("core")
+    seats = [(y, core, section) for y in range(far) for core in range(cores) for section in range(sections)]
     moves = [
-        ((section + y) % far * sections + section, y * sections + section)
-        for y in range(far)
-        for section in range(sections)
+        (((section + 2 * core + y) % far * cores + core) * sections + section, (y * cores + core) * sections + section)
+        for y, core, section in seats
     ]
-    tied = lax.ppermute(tied, ("y_hi", "section"), moves)
+    span = len(seats)
+    across = [
+        ((e ^ experts // 2) * span + source, e * span + target) for e in range(experts) for source, target in moves
+    ]
+    weights = lax.ppermute(tied, ("y_hi", "core", "section"), moves)
+    other = lax.ppermute(proj_hidden, ("expert", "y_hi", "core", "section"), across)
 
     sent = call(
         pack_kernel, (holders, pairs + toks // 2, chunk), BF16,
         lax.axis_index("y_hi").reshape(1), active[0].reshape(pairs, hidden), out_grad[0], routes[0].T,
     )
-    tied, sent = lax.optimization_barrier((tied, sent))
     got = exchange(sent, GROUP)
 
-    weights, model = tied[None, :, :chunk], tied[:, chunk:]
-    order = [0]
-    bit = experts // 2
+    weights, model = weights[None, :, :chunk], weights[:, chunk:]
+    weights = jnp.concatenate([weights, other], axis=0)
+    order = [0, experts // 2]
+    bit = experts // 4
     while bit:
         other = lax.ppermute(weights, "expert", [(i, i ^ bit) for i in range(experts)])
         weights = jnp.concatenate([weights, other], axis=0)
@@ -249,9 +255,11 @@
     belongs = (place[:, None] == (jnp.arange(LANES) % CAP)[None, :]).astype(BF16)
     pair_seq = jnp.repeat(seq_ids, top).astype(BF16)
     line = dot(member * pair_seq[:, None], belongs, ((0,), (0,)))
-    slots = call(slots_kernel, (experts, far, CAP + 8, LANES), BF16, parts, route_weight[0], pick, line)
+    slots = call(slots_kernel, (experts, 1, CAP + 8, LANES), BF16, parts, route_weight[0], pick, line)
     near_q = [q] + [lax.ppermute(q, CLOSE, [(i, i ^ k) for i in range(near)]) for k in range(1, near)]
-    known = exchange(slots.reshape(experts * far, CAP + 8, LANES), ("expert", "y_hi"))
+    moved = exchange(slots.reshape(experts, CAP + 8, LANES), "expert")
+    copies = jnp.broadcast_to(moved[None], (far,) + moved.shape)
+    known = exchange(copies.reshape((far * experts,) + moved.shape[1:]), "y_hi")
 
     lines = SEQS // experts
     scores = pl.pallas_call(

time: 122 us -> 124 us (1.016)
  starting transfers between devices: 59.4 us -> 51.3 us
  blocking collectives: 20.6 us -> 27.6 us
  waiting for transfers between devices: 27.9 us -> 32.8 us
  other arithmetic: 2.7 us -> 1.02 us
    ppermute x1 -> x2, starting transfers between devices: 0.65 us -> 14.2 us  [the longest x1 11.6 us: scores_of(): lax.ppermute(proj_hidden, ('expert', 'y_hi', 'core', 'section'), across)]
    ppermute x3 -> x2, starting transfers between devices: 18.2 us -> 5.95 us  [scores_of(): lax.ppermute(weights, 'expert', [(i, i ^ bit) for i in range(experts)])]
    ppermute x1 -> x2, waiting for transfers between devices: 0.01 us -> 11.7 us  [the longest x1 6.57 us: scores_of(): weights = lax.ppermute(tied, ('y_hi', 'core', 'section'), moves)]
    all_to_all x3, starting transfers between devices: 32.4 us -> 21.6 us  [exchange(): return lax.all_to_all(x, axes, split_axis=0, concat_axis=0, tiled=True)]
    all_to_all x1 -> x2, blocking collectives: 20.6 us -> 27.6 us  [exchange(): return lax.all_to_all(x, axes, split_axis=0, concat_axis=0, tiled=True)]
    ppermute x3 -> x2, waiting for transfers between devices: 14.6 us -> 8.19 us  [scores_of(): lax.ppermute(weights, 'expert', [(i, i ^ bit) for i in range(experts)])]
    ppermute x3, starting transfers between devices: 8.16 us -> 9.53 us  [scores_of(): lax.ppermute(q, CLOSE, [(i, i ^ k) for i in range(near)])]
  transfers between devices with their start and end apart: 10 -> 10, of which waited for: 6 -> 7; matrix products, arithmetic and copies ran while one was open for 3% -> 2% of each run, Pallas kernels for 1% -> 0%
where the time goes in v5:
time: 124 us; the launch traced here: 123 us
  starting transfers between devices  51.3 us (41%)
  waiting for transfers between devices  32.8 us (26%)
  blocking collectives  27.6 us (22%)
  Pallas kernels  6.29 us (5%)
  local copies, waits for them, and re-layouts  3.62 us (3%)
    all_to_all x2, blocking collectives, exchange(): return lax.all_to_all(x, axes, split_axis=0, concat_axis=0, tiled=True)  27.6 us
    all_to_all x3, starting transfers between devices, exchange(): return lax.all_to_all(x, axes, split_axis=0, concat_axis=0, tiled=True)  21.6 us
    ppermute x1, starting transfers between devices, scores_of(): lax.ppermute(proj_hidden, ('expert', 'y_hi', 'core', 'section'), across)  11.6 us
    ppermute x3, starting transfers between devices, scores_of(): lax.ppermute(q, CLOSE, [(i, i ^ k) for i in range(near)])  9.53 us
    all_to_all x3, waiting for transfers between devices, exchange(): return lax.all_to_all(x, axes, split_axis=0, concat_axis=0, tiled=True)  8.55 us
    ppermute x2, waiting for transfers between devices, scores_of(): lax.ppermute(weights, 'expert', [(i, i ^ bit) for i in range(experts)])  8.19 us
    ppermute x1, waiting for transfers between devices, scores_of(): weights = lax.ppermute(tied, ('y_hi', 'core', 'section'), moves)  6.57 us
    ppermute x2, starting transfers between devices, scores_of(): lax.ppermute(weights, 'expert', [(i, i ^ bit) for i in range(experts)])  5.95 us
  transfers between devices with their start and end apart: 10, of which 7 were waited for; matrix products, arithmetic and copies ran while one was open for 2% of the time, Pallas kernels for 0%

profile of v5, /device:TPU:1, one launch (start us, length us, event | category | flops | bytes accessed | tf_op | source)
XLA Modules:
  0.0 123.4 jit_solution(8869304180943436747)
XLA Ops:
  0.0 0.0 copy-start
  0.0 0.0 copy-start.1
  0.0 1.5 %reshape_squeeze.9.acts_ref = bf16[64,8192]{1,0:T(8,128)(2,1)S(1)} reshape(bf16[1,32,2,8192]{3,2,1,0:T(2,128)(2,1)} %param.9) | data formatting | bytes 2097152 | tf_op jit(solution)/shard_map/reshape;squeeze | solution.py:224
  1.5 0.0 copy-done
  1.5 0.0 copy-done.1
  1.5 1.2 %shard_map.91 = bf16[16,80,512]{2,1,0:T(8,128)(2,1)} custom-call(s32[1]{0:T(128)} %bitcast.2.turn_ref, bf16[64,8192]{1,0:T(8,128)(2,1)S(1)} %reshape_squeeze.9.acts_ref, bf16[32,3072]{1,0:T(8,128)(2,1)S(1)} %bitcast.30, s32[2,32]{1,0:T(2,128)S(1)} %bitcast.31), custom_call_target="tpu_custom_call" | custom-call | tf_op jit(solution)/shard_map/pallas_call | solution.py:36
  2.8 0.0 copy-start.3
  2.8 0.0 copy-start.4
  2.8 10.5 %all-to-all-start = ((bf16[16,80,512]{2,1,0:T(8,128)(2,1)}), bf16[16,80,512]{2,1,0:T(8,128)(2,1)S(1)}, u32[]{:S(2)}, u32[]{:S(2)}) async-start(bf16[16,80,512]{2,1,0:T(8,128)(2,1)} %shard_map.91), calls=%async_computation | async-start | bytes 2621440 | tf_op jit(solution)/shard_map/all_to_all | solution.py:23
  13.3 0.0 copy-done.3
  13.3 0.0 copy-start.7
  13.3 0.0 copy-start.2
  13.3 0.0 copy-start.5
  13.3 0.0 copy-start.6
  13.3 11.6 %collective-permute-start.1 = (bf16[1,64,512]{2,1,0:T(8,128)(2,1)S(1)}, bf16[1,64,512]{2,1,0:T(8,128)(2,1)S(1)}, u32[]{:S(2)}, u32[]{:S(2)}) collective-permute-start(bf16[1,64,512]{2,1,0:T(8,128)(2,1)S(1)} %copy-done.3), channel_id=1, source_target_pairs={{256,0},{273,1},{290,2},{307,3},{292,4},{309,5},{262,6},{279,7},{2... | collective-permute-start | bytes 196616 | tf_op jit(solution)/shard_map/ppermute | solution.py:220
  24.9 0.0 copy-done.4
  24.9 0.1 pad_select_fusion
  25.0 2.6 %collective-permute-start = (bf16[64,768]{1,0:T(8,128)(2,1)S(1)}, bf16[64,768]{1,0:T(8,128)(2,1)S(1)}, u32[]{:S(2)}, u32[]{:S(2)}) collective-permute-start(bf16[64,768]{1,0:T(8,128)(2,1)S(1)} %pad_maximum_fusion.3), channel_id=1, source_target_pairs={{0,0},{17,1},{34,2},{51,3},{36,4},{53,5},{6,6},{23,7},{16,16},{33,... | collective-permute-start | bytes 294920 | tf_op jit(solution)/shard_map/ppermute | solution.py:219
  27.7 0.1 copy.15
  27.8 0.1 reshape_squeeze.11
  27.9 0.2 fusion
  28.1 0.1 convert_element_type.39
  28.2 0.1 copy.16
  28.3 6.6 %collective-permute-done = bf16[64,768]{1,0:T(8,128)(2,1)S(1)} collective-permute-done((bf16[64,768]{1,0:T(8,128)(2,1)S(1)}, bf16[64,768]{1,0:T(8,128)(2,1)S(1)}, u32[]{:S(2)}, u32[]{:S(2)}) %collective-permute-start) | collective-permute-done | bytes 98336 | tf_op jit(solution)/shard_map/ppermute | solution.py:219
  34.9 5.1 %collective-permute-done.1 = bf16[1,64,512]{2,1,0:T(8,128)(2,1)S(1)} collective-permute-done((bf16[1,64,512]{2,1,0:T(8,128)(2,1)S(1)}, bf16[1,64,512]{2,1,0:T(8,128)(2,1)S(1)}, u32[]{:S(2)}, u32[]{:S(2)}) %collective-permute-start.1) | collective-permute-done | bytes 65568 | tf_op jit(solution)/shard_map/ppermute | solution.py:220
  40.0 4.0 %collective-permute-start.2 = (bf16[2,64,512]{2,1,0:T(8,128)(2,1)S(1)}, bf16[2,64,512]{2,1,0:T(8,128)(2,1)S(1)}, u32[]{:S(2)}, u32[]{:S(2)}) collective-permute-start(bf16[2,64,512]{2,1,0:T(8,128)(2,1)S(1)} %pad_maximum_fusion.2), channel_id=1, source_target_pairs={{0,128},{64,192},{128,0},{192,64},{256,384},{320,448},{384,256},{4... | collective-permute-start | bytes 393224 | tf_op jit(solution)/shard_map/ppermute | solution.py:233
  44.0 4.0 %collective-permute-done.2 = bf16[2,64,512]{2,1,0:T(8,128)(2,1)S(1)} collective-permute-done((bf16[2,64,512]{2,1,0:T(8,128)(2,1)S(1)}, bf16[2,64,512]{2,1,0:T(8,128)(2,1)S(1)}, u32[]{:S(2)}, u32[]{:S(2)}) %collective-permute-start.2) | collective-permute-done | bytes 131104 | tf_op jit(solution)/shard_map/ppermute | solution.py:233
  48.0 1.9 %collective-permute-start.3 = (bf16[4,64,512]{2,1,0:T(8,128)(2,1)S(1)}, bf16[4,64,512]{2,1,0:T(8,128)(2,1)S(1)}, u32[]{:S(2)}, u32[]{:S(2)}) collective-permute-start(bf16[4,64,512]{2,1,0:T(8,128)(2,1)S(1)} %pad_maximum_fusion.1), channel_id=1, source_target_pairs={{0,64},{64,0},{128,192},{192,128},{256,320},{320,256},{384,448},{4... | collective-permute-start | bytes 786440 | tf_op jit(solution)/shard_map/ppermute | solution.py:233
  50.0 0.0 copy-done.7
  50.0 0.0 copy-done.2
  50.0 0.2 reshape_squeeze.10
  50.2 0.3 copy.14
  50.5 0.0 copy-done.5
  50.5 0.1 copy.17.weight_ref
  50.6 0.1 reshape.58
  50.7 0.0 copy-done.6
  50.7 0.1 broadcast_in_dim.28
  50.8 0.1 convert_element_type.42
  50.9 4.2 %collective-permute-done.3 = bf16[4,64,512]{2,1,0:T(8,128)(2,1)S(1)} collective-permute-done((bf16[4,64,512]{2,1,0:T(8,128)(2,1)S(1)}, bf16[4,64,512]{2,1,0:T(8,128)(2,1)S(1)}, u32[]{:S(2)}, u32[]{:S(2)}) %collective-permute-start.3) | collective-permute-done | bytes 262176 | tf_op jit(solution)/shard_map/ppermute | solution.py:233
  55.1 0.1 pad_maximum_fusion
  55.2 0.0 all-to-all-done.got_ref
  55.2 2.1 %shard_map.92 = f32[16,48,128]{2,1,0:T(8,128)} custom-call(s32[1]{0:T(128)} %bitcast.1.odd_ref, s32[8]{0:T(128)S(1)} %broadcast_xor_fusion.order_ref, bf16[16,80,512]{2,1,0:T(8,128)(2,1)S(1)} %all-to-all-done.got_ref, bf16[512,512]{1,0:T(8,128)(2,1)S(1)} %bitcast.27, bf16[128,256]{1,0:T(8,128)(2,1)S(1)} %pad_maximum_fusion.4.model_ref), custom_call_target="tpu_custom_call" | custom-call | tf_op jit(solution)/shard_map/pallas_call | solution.py:36
  57.3 7.8 %all-to-all-start.1 = ((f32[16,48,128]{2,1,0:T(8,128)}), f32[16,48,128]{2,1,0:T(8,128)S(1)}, u32[]{:S(2)}, u32[]{:S(2)}) async-start(f32[16,48,128]{2,1,0:T(8,128)} %shard_map.92), calls=%async_computation.1 | async-start | bytes 786432 | tf_op jit(solution)/shard_map/all_to_all | solution.py:23
  65.1 0.1 pad_add_fusion
  65.2 0.2 fusion.3.line_ref
  65.4 8.5 %all-to-all-done.1.parts_ref = f32[16,48,128]{2,1,0:T(8,128)S(1)} async-done(((f32[16,48,128]{2,1,0:T(8,128)}), f32[16,48,128]{2,1,0:T(8,128)S(1)}, u32[]{:S(2)}, u32[]{:S(2)}) %all-to-all-start.1) | async-done | bytes 393248 | tf_op jit(solution)/shard_map/all_to_all | solution.py:23
  73.9 0.2 shard_map.93
  74.2 11.0 %all_to_all.25 = bf16[8,24,128]{2,1,0:T(8,128)(2,1)S(1)} all-to-all(bf16[8,24,128]{2,1,0:T(8,128)(2,1)S(1)} %bitcast.29), channel_id=1, replica_groups=mesh['expert'=8,'y_hi'=4,'y_lo'=2,'core'=2,'section'=4] {'expert'}, dimensions={0} | all-to-all | bytes 98304 | tf_op jit(solution)/shard_map/all_to_all | solution.py:23
  85.1 0.7 broadcast_in_dim.29
  85.8 3.4 %all-to-all-start.3 = ((bf16[32,24,128]{2,1,0:T(8,128)(2,1)}), bf16[32,24,128]{2,1,0:T(8,128)(2,1)S(1)}, u32[]{:S(2)}, u32[]{:S(2)}) async-start(bf16[32,24,128]{2,1,0:T(8,128)(2,1)} %bitcast.14), calls=%async_computation.3 | async-start | bytes 393216 | tf_op jit(solution)/shard_map/all_to_all | solution.py:23
  89.2 0.1 copy.21.refs_0_
  89.3 4.1 %collective-permute-start.4 = (bf16[64,1024]{1,0:T(8,128)(2,1)S(1)}, bf16[64,1024]{1,0:T(8,128)(2,1)S(1)}, u32[]{:S(2)}, u32[]{:S(2)}) collective-permute-start(bf16[64,1024]{1,0:T(8,128)(2,1)S(1)} %copy.21.refs_0_), channel_id=1, source_target_pairs={{0,4},{4,0},{8,12},{12,8},{1,5},{5,1},{9,13},{13,9},{2,6},{6,2},{1... | collective-permute-start | bytes 393224 | tf_op jit(solution)/shard_map/ppermute | solution.py:259
  93.4 2.2 %collective-permute-start.5 = (bf16[64,1024]{1,0:T(8,128)(2,1)S(1)}, bf16[64,1024]{1,0:T(8,128)(2,1)S(1)}, u32[]{:S(2)}, u32[]{:S(2)}) collective-permute-start(bf16[64,1024]{1,0:T(8,128)(2,1)S(1)} %copy.21.refs_0_), channel_id=1, source_target_pairs={{0,8},{4,12},{8,0},{12,4},{1,9},{5,13},{9,1},{13,5},{2,10},{6,14},... | collective-permute-start | bytes 393224 | tf_op jit(solution)/shard_map/ppermute | solution.py:259
  95.6 3.3 %collective-permute-start.6 = (bf16[64,1024]{1,0:T(8,128)(2,1)S(1)}, bf16[64,1024]{1,0:T(8,128)(2,1)S(1)}, u32[]{:S(2)}, u32[]{:S(2)}) collective-permute-start(bf16[64,1024]{1,0:T(8,128)(2,1)S(1)} %copy.21.refs_0_), channel_id=1, source_target_pairs={{0,12},{4,8},{8,4},{12,0},{1,13},{5,9},{9,5},{13,1},{2,14},{6,10},... | collective-permute-start | bytes 393224 | tf_op jit(solution)/shard_map/ppermute | solution.py:259
  98.9 0.0 collective-permute-done.4.refs_1_
  98.9 1.4 %collective-permute-done.5.refs_2_ = bf16[64,1024]{1,0:T(8,128)(2,1)S(1)} collective-permute-done((bf16[64,1024]{1,0:T(8,128)(2,1)S(1)}, bf16[64,1024]{1,0:T(8,128)(2,1)S(1)}, u32[]{:S(2)}, u32[]{:S(2)}) %collective-permute-start.5) | collective-permute-done | bytes 131104 | tf_op jit(solution)/shard_map/ppermute | solution.py:259
  100.3 3.0 %collective-permute-done.6.refs_3_ = bf16[64,1024]{1,0:T(8,128)(2,1)S(1)} collective-permute-done((bf16[64,1024]{1,0:T(8,128)(2,1)S(1)}, bf16[64,1024]{1,0:T(8,128)(2,1)S(1)}, u32[]{:S(2)}, u32[]{:S(2)}) %collective-permute-start.6) | collective-permute-done | bytes 131104 | tf_op jit(solution)/shard_map/ppermute | solution.py:259
  103.3 0.0 all-to-all-done.3.known_ref
  103.3 2.7 %score.1 = f32[8,4,8,16]{3,2,1,0:T(8,128)S(1)} custom-call(s32[1]{0:T(128)} %bitcast.mine_ref, bf16[32,24,128]{2,1,0:T(8,128)(2,1)S(1)} %all-to-all-done.3.known_ref, bf16[64,1024]{1,0:T(8,128)(2,1)S(1)} %copy.21.refs_0_, bf16[64,1024]{1,0:T(8,128)(2,1)S(1)} %collective-permute-done.4.refs_1_, bf16[64,1024]{1,0:T(8,128)(2,1)S(1)} %collective-permute-done.5.refs_2_, ...), custom_call_target="tpu_custom_call" | custom-call | tf_op jit(solution)/shard_map/score/pallas_call | solution.py:265
  106.1 16.6 %all_to_all.26 = f32[128,2,16]{2,1,0:T(2,128)S(1)} all-to-all(f32[128,2,16]{2,1,0:T(2,128)S(1)} %bitcast.28), channel_id=1, replica_groups=mesh['expert'=8,'y_hi'=4,'y_lo'=2,'core'=2,'section'=4] {'expert','y_lo'..., dimensions={0} | all-to-all | bytes 32768 | tf_op jit(solution)/shard_map/all_to_all | solution.py:23
  122.7 0.7 reduce_sum.19
  (14 shorter events, 0.1 us)
Async XLA Ops:
  0.0 1.5 %copy-start = (bf16[1,32,3072]{2,1,0:T(8,128)(2,1)S(1)}, bf16[1,32,3072]{2,1,0:T(8,128)(2,1)}, u32[]{:S(2)}) copy-start(bf16[1,32,3072]{2,1,0:T(8,128)(2,1)} %param.10) | copy-start | bytes 589828
  0.0 1.5 %copy-start.1 = (s32[1,32,2]{1,2,0:T(2,128)S(1)}, s32[1,32,2]{1,2,0:T(2,128)}, u32[]{:S(2)}) copy-start(s32[1,32,2]{1,2,0:T(2,128)} %param.12) | copy-start | bytes 772
  2.8 10.5 %copy-start.3 = (bf16[1,64,512]{2,1,0:T(8,128)(2,1)S(1)}, bf16[1,64,512]{2,1,0:T(8,128)(2,1)}, u32[]{:S(2)}) copy-start(bf16[1,64,512]{2,1,0:T(8,128)(2,1)} %param.15) | copy-start | bytes 196612
  2.8 22.2 %copy-start.4 = (bf16[64,192]{1,0:T(8,128)(2,1)S(1)}, bf16[64,192]{1,0:T(8,128)(2,1)}, u32[]{:S(2)}) copy-start(bf16[64,192]{1,0:T(8,128)(2,1)} %param.11) | copy-start | bytes 73732
  2.8 52.4 %all-to-all-start = ((bf16[16,80,512]{2,1,0:T(8,128)(2,1)}), bf16[16,80,512]{2,1,0:T(8,128)(2,1)S(1)}, u32[]{:S(2)}, u32[]{:S(2)}) async-start(bf16[16,80,512]{2,1,0:T(8,128)(2,1)} %shard_map.91), calls=%async_computation | async-start | bytes 2621440 | tf_op jit(solution)/shard_map/all_to_all | solution.py:23
  13.3 36.7 %copy-start.7 = (s32[8]{0:T(128)S(1)}, s32[8]{0:T(128)}, u32[]{:S(2)}) copy-start(s32[8]{0:T(128)} %constant.55.clone) | copy-start | bytes 100
  13.3 36.7 %copy-start.2 = (bf16[1,1,16,4096]{3,2,1,0:T(8,128)(2,1)S(1)}, bf16[1,1,16,4096]{3,2,1,0:T(8,128)(2,1)}, u32[]{:S(2)}) copy-start(bf16[1,1,16,4096]{3,2,1,0:T(8,128)(2,1)} %param.16) | copy-start | bytes 393220
  13.3 37.2 %copy-start.5 = (f32[1,32,2]{1,2,0:T(2,128)S(1)}, f32[1,32,2]{1,2,0:T(2,128)}, u32[]{:S(2)}) copy-start(f32[1,32,2]{1,2,0:T(2,128)} %param.13) | copy-start | bytes 772
  13.3 37.4 %copy-start.6 = (s32[32]{0:T(128)S(1)}, s32[32]{0:T(128)}, u32[]{:S(2)}) copy-start(s32[32]{0:T(128)} %param.14) | copy-start | bytes 388
  13.3 26.6 %collective-permute-start.1 = (bf16[1,64,512]{2,1,0:T(8,128)(2,1)S(1)}, bf16[1,64,512]{2,1,0:T(8,128)(2,1)S(1)}, u32[]{:S(2)}, u32[]{:S(2)}) collective-permute-start(bf16[1,64,512]{2,1,0:T(8,128)(2,1)S(1)} %copy-done.3), channel_id=1, source_target_pairs={{256,0},{273,1},{290,2},{307,3},{292,4},{309,5},{262,6},{279,7},{2... | collective-permute-start | bytes 196616 | tf_op jit(solution)/shard_map/ppermute | solution.py:220
  25.0 9.8 %collective-permute-start = (bf16[64,768]{1,0:T(8,128)(2,1)S(1)}, bf16[64,768]{1,0:T(8,128)(2,1)S(1)}, u32[]{:S(2)}, u32[]{:S(2)}) collective-permute-start(bf16[64,768]{1,0:T(8,128)(2,1)S(1)} %pad_maximum_fusion.3), channel_id=1, source_target_pairs={{0,0},{17,1},{34,2},{51,3},{36,4},{53,5},{6,6},{23,7},{16,16},{33,... | collective-permute-start | bytes 294920 | tf_op jit(solution)/shard_map/ppermute | solution.py:219
  40.0 8.0 %collective-permute-start.2 = (bf16[2,64,512]{2,1,0:T(8,128)(2,1)S(1)}, bf16[2,64,512]{2,1,0:T(8,128)(2,1)S(1)}, u32[]{:S(2)}, u32[]{:S(2)}) collective-permute-start(bf16[2,64,512]{2,1,0:T(8,128)(2,1)S(1)} %pad_maximum_fusion.2), channel_id=1, source_target_pairs={{0,128},{64,192},{128,0},{192,64},{256,384},{320,448},{384,256},{4... | collective-permute-start | bytes 393224 | tf_op jit(solution)/shard_map/ppermute | solution.py:233
  48.0 7.1 %collective-permute-start.3 = (bf16[4,64,512]{2,1,0:T(8,128)(2,1)S(1)}, bf16[4,64,512]{2,1,0:T(8,128)(2,1)S(1)}, u32[]{:S(2)}, u32[]{:S(2)}) collective-permute-start(bf16[4,64,512]{2,1,0:T(8,128)(2,1)S(1)} %pad_maximum_fusion.1), channel_id=1, source_target_pairs={{0,64},{64,0},{128,192},{192,128},{256,320},{320,256},{384,448},{4... | collective-permute-start | bytes 786440 | tf_op jit(solution)/shard_map/ppermute | solution.py:233
  57.3 16.6 %all-to-all-start.1 = ((f32[16,48,128]{2,1,0:T(8,128)}), f32[16,48,128]{2,1,0:T(8,128)S(1)}, u32[]{:S(2)}, u32[]{:S(2)}) async-start(f32[16,48,128]{2,1,0:T(8,128)} %shard_map.92), calls=%async_computation.1 | async-start | bytes 786432 | tf_op jit(solution)/shard_map/all_to_all | solution.py:23
  85.8 17.5 %all-to-all-start.3 = ((bf16[32,24,128]{2,1,0:T(8,128)(2,1)}), bf16[32,24,128]{2,1,0:T(8,128)(2,1)S(1)}, u32[]{:S(2)}, u32[]{:S(2)}) async-start(bf16[32,24,128]{2,1,0:T(8,128)(2,1)} %bitcast.14), calls=%async_computation.3 | async-start | bytes 393216 | tf_op jit(solution)/shard_map/all_to_all | solution.py:23
  89.3 9.6 %collective-permute-start.4 = (bf16[64,1024]{1,0:T(8,128)(2,1)S(1)}, bf16[64,1024]{1,0:T(8,128)(2,1)S(1)}, u32[]{:S(2)}, u32[]{:S(2)}) collective-permute-start(bf16[64,1024]{1,0:T(8,128)(2,1)S(1)} %copy.21.refs_0_), channel_id=1, source_target_pairs={{0,4},{4,0},{8,12},{12,8},{1,5},{5,1},{9,13},{13,9},{2,6},{6,2},{1... | collective-permute-start | bytes 393224 | tf_op jit(solution)/shard_map/ppermute | solution.py:259
  93.4 6.9 %collective-permute-start.5 = (bf16[64,1024]{1,0:T(8,128)(2,1)S(1)}, bf16[64,1024]{1,0:T(8,128)(2,1)S(1)}, u32[]{:S(2)}, u32[]{:S(2)}) collective-permute-start(bf16[64,1024]{1,0:T(8,128)(2,1)S(1)} %copy.21.refs_0_), channel_id=1, source_target_pairs={{0,8},{4,12},{8,0},{12,4},{1,9},{5,13},{9,1},{13,5},{2,10},{6,14},... | collective-permute-start | bytes 393224 | tf_op jit(solution)/shard_map/ppermute | solution.py:259
  95.6 7.7 %collective-permute-start.6 = (bf16[64,1024]{1,0:T(8,128)(2,1)S(1)}, bf16[64,1024]{1,0:T(8,128)(2,1)S(1)}, u32[]{:S(2)}, u32[]{:S(2)}) collective-permute-start(bf16[64,1024]{1,0:T(8,128)(2,1)S(1)} %copy.21.refs_0_), channel_id=1, source_target_pairs={{0,12},{4,8},{8,4},{12,0},{1,13},{5,9},{9,5},{13,1},{2,14},{6,10},... | collective-permute-start | bytes 393224 | tf_op jit(solution)/shard_map/ppermute | solution.py:259

commit v6 on v5

--- a/solution.py
+++ b/solution.py
@@ -201,11 +201,6 @@
     me = lax.axis_index("expert")
     odd = lax.axis_index("core")
 
-    gap = 2 * LANES - width
-    model = jnp.where(
-        odd == 1, jnp.pad(proj_model, ((0, 0), (gap, 0))), jnp.pad(proj_model, ((0, 0), (0, gap)))
-    )
-    tied = jnp.concatenate([proj_hidden[0], model], axis=1)
     cores = lax.axis_size("core")
     seats = [(y, core, section) for y in range(far) for core in range(cores) for section in range(sections)]
     moves = [
@@ -216,7 +211,7 @@
     across = [
         ((e ^ experts // 2) * span + source, e * span + target) for e in range(experts) for source, target in moves
     ]
-    weights = lax.ppermute(tied, ("y_hi", "core", "section"), moves)
+    weights = lax.ppermute(proj_hidden, ("y_hi", "core", "section"), moves)
     other = lax.ppermute(proj_hidden, ("expert", "y_hi", "core", "section"), across)
 
     sent = call(
@@ -225,7 +220,6 @@
     )
     got = exchange(sent, GROUP)
 
-    weights, model = weights[None, :, :chunk], weights[:, chunk:]
     weights = jnp.concatenate([weights, other], axis=0)
     order = [0, experts // 2]
     bit = experts // 4
@@ -234,6 +228,11 @@
         weights = jnp.concatenate([weights, other], axis=0)
         order = order + [o ^ bit for o in order]
         bit //= 2
+    gap = 2 * LANES - width
+    model = jnp.where(
+        odd == 1, jnp.pad(proj_model, ((0, 0), (gap, 0))), jnp.pad(proj_model, ((0, 0), (0, gap)))
+    )
+    model = lax.ppermute(model, ("y_hi", "core", "section"), moves)
     named = me ^ jnp.array(order, jnp.int32)
     model = jnp.concatenate([model, model], axis=0)
     partial = call(
@@ -255,11 +254,9 @@
     belongs = (place[:, None] == (jnp.arange(LANES) % CAP)[None, :]).astype(BF16)
     pair_seq = jnp.repeat(seq_ids, top).astype(BF16)
     line = dot(member * pair_seq[:, None], belongs, ((0,), (0,)))
-    slots = call(slots_kernel, (experts, 1, CAP + 8, LANES), BF16, parts, route_weight[0], pick, line)
+    slots = call(slots_kernel, (experts, far, CAP + 8, LANES), BF16, parts, route_weight[0], pick, line)
     near_q = [q] + [lax.ppermute(q, CLOSE, [(i, i ^ k) for i in range(near)]) for k in range(1, near)]
-    moved = exchange(slots.reshape(experts, CAP + 8, LANES), "expert")
-    copies = jnp.broadcast_to(moved[None], (far,) + moved.shape)
-    known = exchange(copies.reshape((far * experts,) + moved.shape[1:]), "y_hi")
+    known = exchange(slots.reshape(experts * far, CAP + 8, LANES), ("expert", "y_hi"))
 
     lines = SEQS // experts
     scores = pl.pallas_call(

time: 124 us -> 118 us (0.952)
  starting transfers between devices: 51.3 us -> 58.8 us
  blocking collectives: 27.6 us -> 20.6 us
  waiting for transfers between devices: 32.8 us -> 26.9 us
    all_to_all x2 -> x1, blocking collectives: 27.6 us -> 20.6 us  [exchange(): return lax.all_to_all(x, axes, split_axis=0, concat_axis=0, tiled=True)]
    ppermute x1 -> x2, waiting for transfers between devices: 6.57 us -> 0.01 us  [the longest x1 0.01 us: scores_of(): weights = lax.ppermute(proj_hidden, ('y_hi', 'core', 'section'), moves)]
    ppermute x1 -> x2, starting transfers between devices: 2.64 us -> 9.18 us  [the longest x1 6.54 us: scores_of(): model = lax.ppermute(model, ('y_hi', 'core', 'section'), moves)]
    all_to_all x3, starting transfers between devices: 21.6 us -> 24.1 us  [exchange(): return lax.all_to_all(x, axes, split_axis=0, concat_axis=0, tiled=True)]
    ppermute x3, starting transfers between devices: 9.53 us -> 8.16 us  [scores_of(): lax.ppermute(q, CLOSE, [(i, i ^ k) for i in range(near)])]
  transfers between devices with their start and end apart: 10 -> 11, of which waited for: 7 -> 6; matrix products, arithmetic and copies ran while one was open for 2% -> 2% of each run, Pallas kernels for 0% -> 0%
where the time goes in v6:
time: 118 us
  starting transfers between devices  58.8 us (50%)
  waiting for transfers between devices  26.9 us (23%)
  blocking collectives  20.6 us (17%)
  Pallas kernels  6.99 us (6%)
  local copies, waits for them, and re-layouts  2.9 us (2%)
    all_to_all x3, starting transfers between devices, exchange(): return lax.all_to_all(x, axes, split_axis=0, concat_axis=0, tiled=True)  24.1 us
    all_to_all x1, blocking collectives, exchange(): return lax.all_to_all(x, axes, split_axis=0, concat_axis=0, tiled=True)  20.6 us
    ppermute x1, starting transfers between devices, scores_of(): lax.ppermute(proj_hidden, ('expert', 'y_hi', 'core', 'section'), across)  11.5 us
    all_to_all x3, waiting for transfers between devices, exchange(): return lax.all_to_all(x, axes, split_axis=0, concat_axis=0, tiled=True)  8.55 us
    ppermute x2, waiting for transfers between devices, scores_of(): lax.ppermute(weights, 'expert', [(i, i ^ bit) for i in range(experts)])  8.23 us
    ppermute x3, starting transfers between devices, scores_of(): lax.ppermute(q, CLOSE, [(i, i ^ k) for i in range(near)])  8.16 us
    ppermute x1, starting transfers between devices, scores_of(): model = lax.ppermute(model, ('y_hi', 'core', 'section'), moves)  6.54 us
    ppermute x2, starting transfers between devices, scores_of(): lax.ppermute(weights, 'expert', [(i, i ^ bit) for i in range(experts)])  5.91 us
  transfers between devices with their start and end apart: 11, of which 6 were waited for; matrix products, arithmetic and copies ran while one was open for 2% of the time, Pallas kernels for 0%

profile of v6, /device:TPU:1, one launch (start us, length us, event | category | flops | bytes accessed | tf_op | source)
XLA Modules:
  0.0 117.8 jit_solution(2616776453746708663)
XLA Ops:
  0.0 0.0 copy-start
  0.0 0.0 copy-start.1
  0.0 1.5 %reshape_squeeze.9.acts_ref = bf16[64,8192]{1,0:T(8,128)(2,1)S(1)} reshape(bf16[1,32,2,8192]{3,2,1,0:T(2,128)(2,1)} %param.9) | data formatting | bytes 2097152 | tf_op jit(solution)/shard_map/reshape;squeeze | solution.py:219
  1.5 0.0 copy-done
  1.5 0.0 copy-done.1
  1.5 1.2 %shard_map.91 = bf16[16,80,512]{2,1,0:T(8,128)(2,1)} custom-call(s32[1]{0:T(128)} %bitcast.2.turn_ref, bf16[64,8192]{1,0:T(8,128)(2,1)S(1)} %reshape_squeeze.9.acts_ref, bf16[32,3072]{1,0:T(8,128)(2,1)S(1)} %bitcast.25, s32[2,32]{1,0:T(2,128)S(1)} %bitcast.26), custom_call_target="tpu_custom_call" | custom-call | tf_op jit(solution)/shard_map/pallas_call | solution.py:36
  2.8 0.0 copy-start.5
  2.8 0.0 copy-start.3
  2.8 0.0 copy-start.7
  2.8 0.0 copy-start.2
  2.8 10.5 %all-to-all-start = ((bf16[16,80,512]{2,1,0:T(8,128)(2,1)}), bf16[16,80,512]{2,1,0:T(8,128)(2,1)S(1)}, u32[]{:S(2)}, u32[]{:S(2)}) async-start(bf16[16,80,512]{2,1,0:T(8,128)(2,1)} %shard_map.91), calls=%async_computation | async-start | bytes 2621440 | tf_op jit(solution)/shard_map/all_to_all | solution.py:23
  13.3 0.0 copy-done.5
  13.3 0.0 copy-start.4
  13.3 0.0 copy-start.6
  13.3 11.5 %collective-permute-start.1 = (bf16[1,64,512]{2,1,0:T(8,128)(2,1)S(1)}, bf16[1,64,512]{2,1,0:T(8,128)(2,1)S(1)}, u32[]{:S(2)}, u32[]{:S(2)}) collective-permute-start(bf16[1,64,512]{2,1,0:T(8,128)(2,1)S(1)} %copy-done.5), channel_id=1, source_target_pairs={{256,0},{273,1},{290,2},{307,3},{292,4},{309,5},{262,6},{279,7},{2... | collective-permute-start | bytes 196616 | tf_op jit(solution)/shard_map/ppermute | solution.py:215
  24.8 2.6 %collective-permute-start = (bf16[1,64,512]{2,1,0:T(8,128)(2,1)S(1)}, bf16[1,64,512]{2,1,0:T(8,128)(2,1)S(1)}, u32[]{:S(2)}, u32[]{:S(2)}) collective-permute-start(bf16[1,64,512]{2,1,0:T(8,128)(2,1)S(1)} %copy-done.5), channel_id=1, source_target_pairs={{0,0},{17,1},{34,2},{51,3},{36,4},{53,5},{6,6},{23,7},{16,16},{33,... | collective-permute-start | bytes 196616 | tf_op jit(solution)/shard_map/ppermute | solution.py:214
  27.4 0.0 copy-done.3
  27.4 0.1 pad_select_fusion
  27.5 6.5 %collective-permute-start.4 = (bf16[64,256]{1,0:T(8,128)(2,1)S(1)}, bf16[64,256]{1,0:T(8,128)(2,1)S(1)}, u32[]{:S(2)}, u32[]{:S(2)}) collective-permute-start(bf16[64,256]{1,0:T(8,128)(2,1)S(1)} %pad_select_fusion), channel_id=1, source_target_pairs={{0,0},{17,1},{34,2},{51,3},{36,4},{53,5},{6,6},{23,7},{16,16},{33,... | collective-permute-start | bytes 98312 | tf_op jit(solution)/shard_map/ppermute | solution.py:235
  34.1 0.1 copy.15
  34.2 0.1 reshape_squeeze.11
  34.3 0.2 fusion
  34.5 0.1 convert_element_type.39
  34.6 0.1 copy.16
  34.7 5.4 %collective-permute-done.1 = bf16[1,64,512]{2,1,0:T(8,128)(2,1)S(1)} collective-permute-done((bf16[1,64,512]{2,1,0:T(8,128)(2,1)S(1)}, bf16[1,64,512]{2,1,0:T(8,128)(2,1)S(1)}, u32[]{:S(2)}, u32[]{:S(2)}) %collective-permute-start.1) | collective-permute-done | bytes 65568 | tf_op jit(solution)/shard_map/ppermute | solution.py:215
  40.0 0.0 collective-permute-done
  40.1 4.0 %collective-permute-start.2 = (bf16[2,64,512]{2,1,0:T(8,128)(2,1)S(1)}, bf16[2,64,512]{2,1,0:T(8,128)(2,1)S(1)}, u32[]{:S(2)}, u32[]{:S(2)}) collective-permute-start(bf16[2,64,512]{2,1,0:T(8,128)(2,1)S(1)} %pad_maximum_fusion.2), channel_id=1, source_target_pairs={{0,128},{64,192},{128,0},{192,64},{256,384},{320,448},{384,256},{4... | collective-permute-start | bytes 393224 | tf_op jit(solution)/shard_map/ppermute | solution.py:227
  44.1 4.0 %collective-permute-done.2 = bf16[2,64,512]{2,1,0:T(8,128)(2,1)S(1)} collective-permute-done((bf16[2,64,512]{2,1,0:T(8,128)(2,1)S(1)}, bf16[2,64,512]{2,1,0:T(8,128)(2,1)S(1)}, u32[]{:S(2)}, u32[]{:S(2)}) %collective-permute-start.2) | collective-permute-done | bytes 131104 | tf_op jit(solution)/shard_map/ppermute | solution.py:227
  48.1 1.9 %collective-permute-start.3 = (bf16[4,64,512]{2,1,0:T(8,128)(2,1)S(1)}, bf16[4,64,512]{2,1,0:T(8,128)(2,1)S(1)}, u32[]{:S(2)}, u32[]{:S(2)}) collective-permute-start(bf16[4,64,512]{2,1,0:T(8,128)(2,1)S(1)} %pad_maximum_fusion.1), channel_id=1, source_target_pairs={{0,64},{64,0},{128,192},{192,128},{256,320},{320,256},{384,448},{4... | collective-permute-start | bytes 786440 | tf_op jit(solution)/shard_map/ppermute | solution.py:227
  50.0 0.0 copy-done.7
  50.1 0.0 copy-done.2
  50.1 0.2 reshape_squeeze.10
  50.3 0.3 copy.14
  50.6 0.0 copy-done.4
  50.6 0.1 copy.17.weight_ref
  50.7 0.1 reshape.54
  50.8 0.0 copy-done.6
  50.8 0.1 broadcast_in_dim.18
  50.9 0.1 convert_element_type.42
  51.0 0.0 collective-permute-done.4
  51.0 4.2 %collective-permute-done.3 = bf16[4,64,512]{2,1,0:T(8,128)(2,1)S(1)} collective-permute-done((bf16[4,64,512]{2,1,0:T(8,128)(2,1)S(1)}, bf16[4,64,512]{2,1,0:T(8,128)(2,1)S(1)}, u32[]{:S(2)}, u32[]{:S(2)}) %collective-permute-start.3) | collective-permute-done | bytes 262176 | tf_op jit(solution)/shard_map/ppermute | solution.py:227
  55.2 0.1 pad_maximum_fusion
  55.3 0.0 all-to-all-done.got_ref
  55.3 2.1 %shard_map.92 = f32[16,48,128]{2,1,0:T(8,128)} custom-call(s32[1]{0:T(128)} %bitcast.1.odd_ref, s32[8]{0:T(128)S(1)} %broadcast_xor_fusion.order_ref, bf16[16,80,512]{2,1,0:T(8,128)(2,1)S(1)} %all-to-all-done.got_ref, bf16[512,512]{1,0:T(8,128)(2,1)S(1)} %bitcast.23, bf16[128,256]{1,0:T(8,128)(2,1)S(1)} %pad_maximum_fusion.3.model_ref), custom_call_target="tpu_custom_call" | custom-call | tf_op jit(solution)/shard_map/pallas_call | solution.py:36
  57.4 7.8 %all-to-all-start.1 = ((f32[16,48,128]{2,1,0:T(8,128)}), f32[16,48,128]{2,1,0:T(8,128)S(1)}, u32[]{:S(2)}, u32[]{:S(2)}) async-start(f32[16,48,128]{2,1,0:T(8,128)} %shard_map.92), calls=%async_computation.1 | async-start | bytes 786432 | tf_op jit(solution)/shard_map/all_to_all | solution.py:23
  65.2 0.1 pad_add_fusion
  65.3 0.2 fusion.3.line_ref
  65.5 8.5 %all-to-all-done.1.parts_ref = f32[16,48,128]{2,1,0:T(8,128)S(1)} async-done(((f32[16,48,128]{2,1,0:T(8,128)}), f32[16,48,128]{2,1,0:T(8,128)S(1)}, u32[]{:S(2)}, u32[]{:S(2)}) %all-to-all-start.1) | async-done | bytes 393248 | tf_op jit(solution)/shard_map/all_to_all | solution.py:23
  74.0 0.9 shard_map.93
  75.0 5.8 %all-to-all-start.2 = ((bf16[32,24,128]{2,1,0:T(8,128)(2,1)}), bf16[32,24,128]{2,1,0:T(8,128)(2,1)S(1)}, u32[]{:S(2)}, u32[]{:S(2)}) async-start(bf16[32,24,128]{2,1,0:T(8,128)(2,1)} %bitcast.11), calls=%async_computation.2 | async-start | bytes 393216 | tf_op jit(solution)/shard_map/all_to_all | solution.py:23
  80.8 0.1 copy.21.refs_0_
  80.9 2.7 %collective-permute-start.5 = (bf16[64,1024]{1,0:T(8,128)(2,1)S(1)}, bf16[64,1024]{1,0:T(8,128)(2,1)S(1)}, u32[]{:S(2)}, u32[]{:S(2)}) collective-permute-start(bf16[64,1024]{1,0:T(8,128)(2,1)S(1)} %copy.21.refs_0_), channel_id=1, source_target_pairs={{0,4},{4,0},{8,12},{12,8},{1,5},{5,1},{9,13},{13,9},{2,6},{6,2},{1... | collective-permute-start | bytes 393224 | tf_op jit(solution)/shard_map/ppermute | solution.py:258
  83.6 2.2 %collective-permute-start.6 = (bf16[64,1024]{1,0:T(8,128)(2,1)S(1)}, bf16[64,1024]{1,0:T(8,128)(2,1)S(1)}, u32[]{:S(2)}, u32[]{:S(2)}) collective-permute-start(bf16[64,1024]{1,0:T(8,128)(2,1)S(1)} %copy.21.refs_0_), channel_id=1, source_target_pairs={{0,8},{4,12},{8,0},{12,4},{1,9},{5,13},{9,1},{13,5},{2,10},{6,14},... | collective-permute-start | bytes 393224 | tf_op jit(solution)/shard_map/ppermute | solution.py:258
  85.8 3.3 %collective-permute-start.7 = (bf16[64,1024]{1,0:T(8,128)(2,1)S(1)}, bf16[64,1024]{1,0:T(8,128)(2,1)S(1)}, u32[]{:S(2)}, u32[]{:S(2)}) collective-permute-start(bf16[64,1024]{1,0:T(8,128)(2,1)S(1)} %copy.21.refs_0_), channel_id=1, source_target_pairs={{0,12},{4,8},{8,4},{12,0},{1,13},{5,9},{9,5},{13,1},{2,14},{6,10},... | collective-permute-start | bytes 393224 | tf_op jit(solution)/shard_map/ppermute | solution.py:258
  89.1 0.0 collective-permute-done.5.refs_1_
  89.1 1.4 %collective-permute-done.6.refs_2_ = bf16[64,1024]{1,0:T(8,128)(2,1)S(1)} collective-permute-done((bf16[64,1024]{1,0:T(8,128)(2,1)S(1)}, bf16[64,1024]{1,0:T(8,128)(2,1)S(1)}, u32[]{:S(2)}, u32[]{:S(2)}) %collective-permute-start.6) | collective-permute-done | bytes 131104 | tf_op jit(solution)/shard_map/ppermute | solution.py:258
  90.5 3.3 %collective-permute-done.7.refs_3_ = bf16[64,1024]{1,0:T(8,128)(2,1)S(1)} collective-permute-done((bf16[64,1024]{1,0:T(8,128)(2,1)S(1)}, bf16[64,1024]{1,0:T(8,128)(2,1)S(1)}, u32[]{:S(2)}, u32[]{:S(2)}) %collective-permute-start.7) | collective-permute-done | bytes 131104 | tf_op jit(solution)/shard_map/ppermute | solution.py:258
  93.8 0.0 all-to-all-done.2.known_ref
  93.8 2.7 %score.1 = f32[8,4,8,16]{3,2,1,0:T(8,128)S(1)} custom-call(s32[1]{0:T(128)} %bitcast.mine_ref, bf16[32,24,128]{2,1,0:T(8,128)(2,1)S(1)} %all-to-all-done.2.known_ref, bf16[64,1024]{1,0:T(8,128)(2,1)S(1)} %copy.21.refs_0_, bf16[64,1024]{1,0:T(8,128)(2,1)S(1)} %collective-permute-done.5.refs_1_, bf16[64,1024]{1,0:T(8,128)(2,1)S(1)} %collective-permute-done.6.refs_2_, ...), custom_call_target="tpu_custom_call" | custom-call | tf_op jit(solution)/shard_map/score/pallas_call | solution.py:262
  96.6 20.6 %all_to_all.20 = f32[128,2,16]{2,1,0:T(2,128)S(1)} all-to-all(f32[128,2,16]{2,1,0:T(2,128)S(1)} %bitcast.24), channel_id=1, replica_groups=mesh['expert'=8,'y_hi'=4,'y_lo'=2,'core'=2,'section'=4] {'expert','y_lo'..., dimensions={0} | all-to-all | bytes 32768 | tf_op jit(solution)/shard_map/all_to_all | solution.py:23
  117.1 0.7 reduce_sum.19
  (11 shorter events, 0.1 us)
Async XLA Ops:
  0.0 1.5 %copy-start = (bf16[1,32,3072]{2,1,0:T(8,128)(2,1)S(1)}, bf16[1,32,3072]{2,1,0:T(8,128)(2,1)}, u32[]{:S(2)}) copy-start(bf16[1,32,3072]{2,1,0:T(8,128)(2,1)} %param.10) | copy-start | bytes 589828
  0.0 1.5 %copy-start.1 = (s32[1,32,2]{1,2,0:T(2,128)S(1)}, s32[1,32,2]{1,2,0:T(2,128)}, u32[]{:S(2)}) copy-start(s32[1,32,2]{1,2,0:T(2,128)} %param.12) | copy-start | bytes 772
  2.8 10.5 %copy-start.5 = (bf16[1,64,512]{2,1,0:T(8,128)(2,1)S(1)}, bf16[1,64,512]{2,1,0:T(8,128)(2,1)}, u32[]{:S(2)}) copy-start(bf16[1,64,512]{2,1,0:T(8,128)(2,1)} %param.15) | copy-start | bytes 196612
  2.8 24.7 %copy-start.3 = (bf16[64,192]{1,0:T(8,128)(2,1)S(1)}, bf16[64,192]{1,0:T(8,128)(2,1)}, u32[]{:S(2)}) copy-start(bf16[64,192]{1,0:T(8,128)(2,1)} %param.11) | copy-start | bytes 73732
  2.8 47.3 %copy-start.7 = (s32[8]{0:T(128)S(1)}, s32[8]{0:T(128)}, u32[]{:S(2)}) copy-start(s32[8]{0:T(128)} %constant.55.clone) | copy-start | bytes 100
  2.8 47.3 %copy-start.2 = (bf16[1,1,16,4096]{3,2,1,0:T(8,128)(2,1)S(1)}, bf16[1,1,16,4096]{3,2,1,0:T(8,128)(2,1)}, u32[]{:S(2)}) copy-start(bf16[1,1,16,4096]{3,2,1,0:T(8,128)(2,1)} %param.16) | copy-start | bytes 393220
  2.8 52.5 %all-to-all-start = ((bf16[16,80,512]{2,1,0:T(8,128)(2,1)}), bf16[16,80,512]{2,1,0:T(8,128)(2,1)S(1)}, u32[]{:S(2)}, u32[]{:S(2)}) async-start(bf16[16,80,512]{2,1,0:T(8,128)(2,1)} %shard_map.91), calls=%async_computation | async-start | bytes 2621440 | tf_op jit(solution)/shard_map/all_to_all | solution.py:23
  13.3 37.3 %copy-start.4 = (f32[1,32,2]{1,2,0:T(2,128)S(1)}, f32[1,32,2]{1,2,0:T(2,128)}, u32[]{:S(2)}) copy-start(f32[1,32,2]{1,2,0:T(2,128)} %param.13) | copy-start | bytes 772
  13.3 37.5 %copy-start.6 = (s32[32]{0:T(128)S(1)}, s32[32]{0:T(128)}, u32[]{:S(2)}) copy-start(s32[32]{0:T(128)} %param.14) | copy-start | bytes 388
  13.3 26.7 %collective-permute-start.1 = (bf16[1,64,512]{2,1,0:T(8,128)(2,1)S(1)}, bf16[1,64,512]{2,1,0:T(8,128)(2,1)S(1)}, u32[]{:S(2)}, u32[]{:S(2)}) collective-permute-start(bf16[1,64,512]{2,1,0:T(8,128)(2,1)S(1)} %copy-done.5), channel_id=1, source_target_pairs={{256,0},{273,1},{290,2},{307,3},{292,4},{309,5},{262,6},{279,7},{2... | collective-permute-start | bytes 196616 | tf_op jit(solution)/shard_map/ppermute | solution.py:215
  24.8 15.3 %collective-permute-start = (bf16[1,64,512]{2,1,0:T(8,128)(2,1)S(1)}, bf16[1,64,512]{2,1,0:T(8,128)(2,1)S(1)}, u32[]{:S(2)}, u32[]{:S(2)}) collective-permute-start(bf16[1,64,512]{2,1,0:T(8,128)(2,1)S(1)} %copy-done.5), channel_id=1, source_target_pairs={{0,0},{17,1},{34,2},{51,3},{36,4},{53,5},{6,6},{23,7},{16,16},{33,... | collective-permute-start | bytes 196616 | tf_op jit(solution)/shard_map/ppermute | solution.py:214
  27.5 23.5 %collective-permute-start.4 = (bf16[64,256]{1,0:T(8,128)(2,1)S(1)}, bf16[64,256]{1,0:T(8,128)(2,1)S(1)}, u32[]{:S(2)}, u32[]{:S(2)}) collective-permute-start(bf16[64,256]{1,0:T(8,128)(2,1)S(1)} %pad_select_fusion), channel_id=1, source_target_pairs={{0,0},{17,1},{34,2},{51,3},{36,4},{53,5},{6,6},{23,7},{16,16},{33,... | collective-permute-start | bytes 98312 | tf_op jit(solution)/shard_map/ppermute | solution.py:235
  40.1 8.0 %collective-permute-start.2 = (bf16[2,64,512]{2,1,0:T(8,128)(2,1)S(1)}, bf16[2,64,512]{2,1,0:T(8,128)(2,1)S(1)}, u32[]{:S(2)}, u32[]{:S(2)}) collective-permute-start(bf16[2,64,512]{2,1,0:T(8,128)(2,1)S(1)} %pad_maximum_fusion.2), channel_id=1, source_target_pairs={{0,128},{64,192},{128,0},{192,64},{256,384},{320,448},{384,256},{4... | collective-permute-start | bytes 393224 | tf_op jit(solution)/shard_map/ppermute | solution.py:227
  48.1 7.1 %collective-permute-start.3 = (bf16[4,64,512]{2,1,0:T(8,128)(2,1)S(1)}, bf16[4,64,512]{2,1,0:T(8,128)(2,1)S(1)}, u32[]{:S(2)}, u32[]{:S(2)}) collective-permute-start(bf16[4,64,512]{2,1,0:T(8,128)(2,1)S(1)} %pad_maximum_fusion.1), channel_id=1, source_target_pairs={{0,64},{64,0},{128,192},{192,128},{256,320},{320,256},{384,448},{4... | collective-permute-start | bytes 786440 | tf_op jit(solution)/shard_map/ppermute | solution.py:227
  57.4 16.6 %all-to-all-start.1 = ((f32[16,48,128]{2,1,0:T(8,128)}), f32[16,48,128]{2,1,0:T(8,128)S(1)}, u32[]{:S(2)}, u32[]{:S(2)}) async-start(f32[16,48,128]{2,1,0:T(8,128)} %shard_map.92), calls=%async_computation.1 | async-start | bytes 786432 | tf_op jit(solution)/shard_map/all_to_all | solution.py:23
  75.0 18.9 %all-to-all-start.2 = ((bf16[32,24,128]{2,1,0:T(8,128)(2,1)}), bf16[32,24,128]{2,1,0:T(8,128)(2,1)S(1)}, u32[]{:S(2)}, u32[]{:S(2)}) async-start(bf16[32,24,128]{2,1,0:T(8,128)(2,1)} %bitcast.11), calls=%async_computation.2 | async-start | bytes 393216 | tf_op jit(solution)/shard_map/all_to_all | solution.py:23
  80.9 8.2 %collective-permute-start.5 = (bf16[64,1024]{1,0:T(8,128)(2,1)S(1)}, bf16[64,1024]{1,0:T(8,128)(2,1)S(1)}, u32[]{:S(2)}, u32[]{:S(2)}) collective-permute-start(bf16[64,1024]{1,0:T(8,128)(2,1)S(1)} %copy.21.refs_0_), channel_id=1, source_target_pairs={{0,4},{4,0},{8,12},{12,8},{1,5},{5,1},{9,13},{13,9},{2,6},{6,2},{1... | collective-permute-start | bytes 393224 | tf_op jit(solution)/shard_map/ppermute | solution.py:258
  83.6 6.9 %collective-permute-start.6 = (bf16[64,1024]{1,0:T(8,128)(2,1)S(1)}, bf16[64,1024]{1,0:T(8,128)(2,1)S(1)}, u32[]{:S(2)}, u32[]{:S(2)}) collective-permute-start(bf16[64,1024]{1,0:T(8,128)(2,1)S(1)} %copy.21.refs_0_), channel_id=1, source_target_pairs={{0,8},{4,12},{8,0},{12,4},{1,9},{5,13},{9,1},{13,5},{2,10},{6,14},... | collective-permute-start | bytes 393224 | tf_op jit(solution)/shard_map/ppermute | solution.py:258
  85.8 8.0 %collective-permute-start.7 = (bf16[64,1024]{1,0:T(8,128)(2,1)S(1)}, bf16[64,1024]{1,0:T(8,128)(2,1)S(1)}, u32[]{:S(2)}, u32[]{:S(2)}) collective-permute-start(bf16[64,1024]{1,0:T(8,128)(2,1)S(1)} %copy.21.refs_0_), channel_id=1, source_target_pairs={{0,12},{4,8},{8,4},{12,0},{1,13},{5,9},{9,5},{13,1},{2,14},{6,10},... | collective-permute-start | bytes 393224 | tf_op jit(solution)/shard_map/ppermute | solution.py:258
